TPU v7x, 128 devices: a whole 4x4x4 slice. The times are simulated.
128 devices in a mesh: row: 8 (over z, x_hi), col: 16 (over y, x_lo, core).
Axes of the slice: x: 4 (x_hi: 2, x_lo: 2; x = x_hi * 2 + x_lo), y: 4, z: 4, core: 2. Of those that a mesh axis runs over, the one named last changes fastest.
Arguments:
- interaction: bfloat16 [12288, 6144], P('row', 'col'), may hold values from -0.078125 to 0.078125
- cycle_amps: bfloat16 [6144, 12288], P('row', 'col'), may hold values from -6 to 6
- tile_mask: int32 [16, 8], replicated, may hold values 0 or 1
- virt_perm: int32 [384], replicated, may hold values from 0 to 383, each once
- occ_energy: float32 [32], replicated, may hold values from -2 to -0.5
- virt_energy: float32 [384], replicated, may hold values from 0.2 to 3
- old_amps: bfloat16 [12288, 12288], P(('row', 'col')), may hold values from -6 to 6
Outputs:
- new_amps: float32 [12288, 12288], P(('row', 'col'))
Inputs may be any that keep to these rules, and one draw needn't show every extreme that they name: `tile_mask`: 0 or 1 for each tile. `virt_perm`: each number of 0 to 383 once.
All inputs are finite; a program needn't handle non-finite values.
Results may differ from a plain program's by a relative error of at most 0.0012.
Values may be sent and summed in bfloat16 or wider, within the bound.
A program may use at most 320 MiB of HBM per device.

v0:
```python
import jax
import jax.numpy as jnp
from jax import lax
from jax.sharding import PartitionSpec as P

V = 384
TILE = 768


def accumulate(left_part, right_part):
    return jnp.dot(left_part, right_part, preferred_element_type=jnp.float32)


def on_device(interaction, cycle_amps, tile_mask, virt_perm, occ_energy, virt_energy, old_amps):
    row_count = interaction.shape[0]
    local_cols = interaction.shape[1]
    out_cols = cycle_amps.shape[1]
    row_base = lax.axis_index("row") * row_count
    col_base = lax.axis_index("col") * local_cols
    row_tiles = (row_base + jnp.arange(row_count, dtype=jnp.int32)) // TILE
    col_tiles = (col_base + jnp.arange(local_cols, dtype=jnp.int32)) // TILE
    row_onehot = (
        row_tiles[:, None] == jnp.arange(tile_mask.shape[0], dtype=jnp.int32)[None, :]
    ).astype(jnp.float32)
    col_onehot = (
        col_tiles[:, None] == jnp.arange(tile_mask.shape[1], dtype=jnp.int32)[None, :]
    ).astype(jnp.float32)
    mask_rows = jnp.dot(row_onehot, tile_mask.astype(jnp.float32), precision=lax.Precision.HIGHEST)
    mask_block = jnp.dot(mask_rows, col_onehot.T, precision=lax.Precision.HIGHEST)
    masked = interaction * mask_block.astype(jnp.bfloat16)
    amp_full = lax.all_gather(cycle_amps, "row", axis=0, tiled=True)
    cycle_term = accumulate(lax.all_gather(masked, "col", axis=1, tiled=True), amp_full)
    grid = cycle_term.reshape(row_count // V, V, out_cols // V, V)
    permuted = jnp.take(jnp.take(grid, virt_perm, axis=1), virt_perm, axis=3)
    exchange_term = jnp.transpose(permuted, (0, 3, 2, 1)).reshape(row_count, out_cols)
    combined = (2.0 * cycle_term - exchange_term).astype(jnp.bfloat16)
    slab = lax.all_to_all(combined, "col", split_axis=0, concat_axis=1, tiled=True)
    columns = lax.all_to_all(slab, ("row", "col"), split_axis=1, concat_axis=0, tiled=True)
    paired = slab.astype(jnp.float32) + columns.T.astype(jnp.float32)
    slab_rows = slab.shape[0]
    total_cols = slab.shape[1]
    slab_index = lax.axis_index("row") * lax.axis_size("col") + lax.axis_index("col")
    global_rows = slab_index * slab_rows + jnp.arange(slab_rows, dtype=jnp.int32)
    occ_hit = (global_rows // V)[:, None] == jnp.arange(occ_energy.shape[0], dtype=jnp.int32)[
        None, :
    ]
    virt_hit = (global_rows % V)[:, None] == jnp.arange(V, dtype=jnp.int32)[None, :]
    virt_rows = jnp.sum(jnp.where(virt_hit, virt_energy[None, :], jnp.float32(0.0)), axis=1)
    occ_rows = jnp.sum(jnp.where(occ_hit, occ_energy[None, :], jnp.float32(0.0)), axis=1)
    row_energy = virt_rows - occ_rows
    pair_energy = (virt_energy[None, :] - occ_energy[:, None]).reshape(total_cols)
    denominator = row_energy[:, None] + pair_energy[None, :]
    return old_amps.astype(jnp.float32) + paired / denominator


def solution(mesh):
    placed = (P("row", "col"), P("row", "col"), P(), P(), P(), P(), P(("row", "col"), None))
    return jax.shard_map(
        on_device, mesh=mesh, in_specs=placed, out_specs=P(("row", "col"), None), check_vma=False
    )
```

profile of v0, /device:TPU:3, one launch (start us, length us, event | category | flops | bytes accessed | tf_op | source)
XLA Modules:
  0.0 422.7 jit_solution(10562042217417207527)
XLA Ops:
  6.5 0.0 copy-start.2
  6.5 0.0 all-gather.5.cloned.1.call-start
  6.5 0.7 all-gather.5.cloned.1.call-update
  7.3 0.0 all-gather.3.cloned.1.call-start
  7.4 1.9 fusion.3
  9.2 3.8 fusion.2
  13.1 0.0 all-gather.3.cloned.1.call-update
  13.1 0.0 copy-done.2
  13.1 113.5 %all-gather.5.cloned.1.call-done = bf16[6144,768]{1,0:T(8,128)(2,1)} async-done(((bf16[768,768]{1,0:T(8,128)(2,1)}), bf16[6144,768]{1,0:T(8,128)(2,1)}) %all-gather.5.cloned.1.call-update) | async-done | bytes 9437200 | tf_op jit(solution)/shard_map/all_gather | solution.py:31
  126.6 102.6 %all-gather.3.cloned.1.call-done = bf16[1536,6144]{1,0:T(8,128)(2,1)} async-done(((bf16[1536,384]{1,0:T(8,128)(2,1)}), bf16[1536,6144]{1,0:T(8,128)(2,1)}) %all-gather.3.cloned.1.call-update) | async-done | bytes 18874384 | tf_op jit(solution)/shard_map/all_gather | solution.py:32
  229.2 21.2 %fusion.10 = f32[1536,768]{1,0:T(8,128)} fusion(bf16[1536,6144]{1,0:T(8,128)(2,1)} %all-gather.3.cloned.1.call-done, bf16[6144,768]{1,0:T(8,128)(2,1)} %all-gather.5.cloned.1.call-done), kind=kOutput, calls=%fused_computation.39 | convolution fusion | flops 14495514624 | bytes 33030144 | tf_op jit(solution)/shard_map/dot_general | solution.py:11
  250.4 6.7 %reshape.86 = f32[4,384,2,384]{3,2,1,0:T(2,128)} reshape(f32[1536,768]{1,0:T(8,128)} %fusion.10) | data formatting | bytes 9437184 | tf_op jit(solution)/shard_map/reshape | solution.py:33
  257.2 7.5 %copy.25 = f32[4,384,2,384]{3,0,2,1:T(4,128)} copy(f32[4,384,2,384]{3,2,1,0:T(2,128)} %reshape.86) | data formatting | bytes 9437184 | tf_op jit(solution)/shard_map/reshape | solution.py:33
  264.7 7.9 %gather_fusion = f32[384,4,2,384]{3,1,2,0:T(4,128)} fusion(f32[4,384,2,384]{3,0,2,1:T(4,128)} %copy.25, s32[1024]{0:T(1024)S(1)} %pad_clamp_fusion), kind=kCustom, calls=%fused_computation | custom fusion | bytes 9438720 | tf_op jit(solution)/shard_map/jit(_take)/gather | solution.py:34
  272.5 4.8 %select_bitcast_fusion.1 = f32[4,384,2,384]{3,0,2,1:T(4,128)} fusion(f32[384,4,2,384]{3,1,2,0:T(4,128)} %gather_fusion, pred[384]{0:T(512)(128)(4,1)S(1)} %compare_and_fusion), kind=kLoop, calls=%fused_computation.6 | loop fusion | flops 1179648 | bytes 9437568 | tf_op jit(solution)/shard_map/jit(_take)/select_n | solution.py:34
  277.4 6.7 %copy.26 = f32[4,384,2,384]{1,0,2,3:T(4,128)} copy(f32[4,384,2,384]{3,0,2,1:T(4,128)} %select_bitcast_fusion.1) | data formatting | bytes 9437184 | tf_op jit(solution)/shard_map/jit(_take)/select_n | solution.py:34
  284.0 7.9 %gather_fusion.1 = f32[384,4,384,2]{2,1,3,0:T(4,128)} fusion(f32[4,384,2,384]{1,0,2,3:T(4,128)} %copy.26, s32[1024]{0:T(1024)S(1)} %pad_clamp_fusion), kind=kCustom, calls=%fused_computation.1 | custom fusion | bytes 9438720 | tf_op jit(solution)/shard_map/jit(_take)/gather | solution.py:34
  291.9 3.6 select_bitcast_fusion
  295.5 0.0 slice-start
  295.5 2.4 copy.27
  298.0 0.0 slice-start.1
  298.0 0.3 copy.34
  298.3 0.0 slice-done
  298.3 0.7 slice-done.1
  299.0 0.8 subtract_convert_fusion
  299.8 34.5 %all_to_all.29 = bf16[16,96,768]{2,1,0:T(8,128)(2,1)S(1)} all-to-all(bf16[16,96,768]{2,1,0:T(8,128)(2,1)S(1)} %bitcast.32), channel_id=1, replica_groups=mesh['row'=8,'col'=16] {'col'}, dimensions={0} | all-to-all | bytes 4718592 | tf_op jit(solution)/shard_map/all_to_all | solution.py:37
  334.3 2.7 copy.29
  337.0 6.4 %all_to_all.25 = bf16[96,128,96]{2,1,0:T(8,128)(2,1)} reshape(bf16[96,16,768]{2,1,0:T(8,128)(2,1)} %copy.29) | data formatting | bytes 4718592 | tf_op jit(solution)/shard_map/all_to_all | solution.py:38
  343.4 5.5 %copy.30 = bf16[96,128,96]{2,0,1:T(8,128)(2,1)} copy(bf16[96,128,96]{2,1,0:T(8,128)(2,1)} %all_to_all.25) | data formatting | bytes 4718592 | tf_op jit(solution)/shard_map/all_to_all | solution.py:38
  348.9 0.0 copy-start.1
  348.9 0.0 copy-start.3
  348.9 8.1 %all-to-all-start.1 = ((bf16[96,128,96]{2,0,1:T(8,128)(2,1)}), bf16[96,128,96]{2,0,1:T(8,128)(2,1)}, u32[]{:S(2)}, u32[]{:S(2)}) async-start(bf16[96,128,96]{2,0,1:T(8,128)(2,1)} %copy.30), calls=%async_computation.1 | async-start | bytes 6291456 | tf_op jit(solution)/shard_map/all_to_all | solution.py:38
  357.0 0.0 copy-done.1
  357.0 0.0 copy-done.3
  357.0 0.1 broadcast_subtract_fusion
  357.1 0.1 select_reduce_fusion.1
  357.2 0.2 select_reduce_fusion
  357.4 0.5 convert_bitcast_fusion
  357.9 2.7 copy.33
  360.6 36.5 %all-to-all-done.1 = bf16[96,128,96]{2,0,1:T(8,128)(2,1)} async-done(((bf16[96,128,96]{2,0,1:T(8,128)(2,1)}), bf16[96,128,96]{2,0,1:T(8,128)(2,1)}, u32[]{:S(2)}, u32[]{:S(2)}) %all-to-all-start.1) | async-done | bytes 2359328 | tf_op jit(solution)/shard_map/all_to_all | solution.py:38
  397.1 5.4 %convert_element_type.45 = f32[96,128,96]{2,0,1:T(8,128)} convert(bf16[96,128,96]{2,0,1:T(8,128)(2,1)} %all-to-all-done.1) | non-fusion elementwise | flops 1179648 | bytes 7077888 | tf_op jit(solution)/shard_map/convert_element_type | solution.py:39
  402.5 0.0 copy-start
  402.5 6.4 %copy.32 = f32[12288,96]{0,1:T(8,128)} copy(f32[12288,96]{1,0:T(8,128)} %bitcast.25) | data formatting | bytes 9437184 | tf_op jit(solution)/shard_map/convert_element_type | solution.py:39
  408.9 0.0 copy-done
  408.9 7.0 %fusion.1 = f32[96,12288]{1,0:T(8,128)} fusion(f32[96,12288]{1,0:T(8,128)} %bitcast.30, f32[12288,96]{0,1:T(8,128)} %copy.32, bf16[96,12288]{1,0:T(8,128)(2,1)S(1)} %copy-done, f32[12288]{0:T(1024)S(1)} %sub.56, f32[96]{0:T(128)S(1)} %sub.52), kind=kLoop, calls=%fused_computation.4 | loop fusion | flops 5898240 | bytes 16564608 | tf_op jit(solution)/shard_map/add | solution.py:53
  (9 shorter events, 0.1 us)
Async XLA Ops:
  6.5 6.5 %copy-start.2 = (s32[384]{0:T(512)S(1)}, s32[384]{0:T(512)}, u32[]{:S(2)}) copy-start(s32[384]{0:T(512)} %param.10) | copy-start | bytes 4612
  6.5 120.1 %all-gather.5.cloned.1.call-start = ((), (), s32[]{:S(2)}) async-start(), calls=%async_computation.3 | async-start | bytes 10616832 | tf_op jit(solution)/shard_map/all_gather | solution.py:31
  7.3 222.0 %all-gather.3.cloned.1.call-start = ((), (), s32[]{:S(2)}) async-start(), calls=%async_computation.2 | async-start | bytes 20054016 | tf_op jit(solution)/shard_map/all_gather | solution.py:32
  295.5 2.8 slice-start
  298.0 1.0 slice-start.1
  348.9 8.1 %copy-start.1 = (f32[384]{0:T(512)S(1)}, f32[384]{0:T(512)}, u32[]{:S(2)}) copy-start(f32[384]{0:T(512)} %param.12) | copy-start | bytes 4612
  348.9 8.1 %copy-start.3 = (f32[32]{0:T(128)S(1)}, f32[32]{0:T(128)}, u32[]{:S(2)}) copy-start(f32[32]{0:T(128)} %param.11) | copy-start | bytes 388
  348.9 48.2 %all-to-all-start.1 = ((bf16[96,128,96]{2,0,1:T(8,128)(2,1)}), bf16[96,128,96]{2,0,1:T(8,128)(2,1)}, u32[]{:S(2)}, u32[]{:S(2)}) async-start(bf16[96,128,96]{2,0,1:T(8,128)(2,1)} %copy.30), calls=%async_computation.1 | async-start | bytes 6291456 | tf_op jit(solution)/shard_map/all_to_all | solution.py:38
  402.5 6.4 %copy-start = (bf16[96,12288]{1,0:T(8,128)(2,1)S(1)}, bf16[96,12288]{1,0:T(8,128)(2,1)}, u32[]{:S(2)}) copy-start(bf16[96,12288]{1,0:T(8,128)(2,1)} %param.13) | copy-start | bytes 7077892
Sparse Core Ops, SparseCore 0:
  9.6 116.9 all-gather.4
  128.3 100.9 all-gather.2
where the time goes:
time: 425 us; the launch traced here: 423 us
  waiting for transfers between devices  253 us (60%)
  local copies, waits for them, and re-layouts  63.8 us (15%)
  blocking collectives  34.5 us (8%)
  matrix products  26.9 us (6%)
  other arithmetic  22.4 us (5%)
  between operations  13.6 us (3%)
  starting transfers between devices  8.1 us (2%)
    all_gather x1, waiting for transfers between devices, on_device(): amp_full = lax.all_gather(cycle_amps, 'row', axis=0, tiled=True)  113 us
    all_gather x1, waiting for transfers between devices, on_device(): lax.all_gather(masked, 'col', axis=1, tiled=True)  103 us
    all_to_all x1, waiting for transfers between devices, on_device(): lax.all_to_all(slab, ('row', 'col'), split_axis=1, concat_axis=0, tiled=T...  36.5 us
    all_to_all x1, blocking collectives, on_device(): lax.all_to_all(combined, 'col', split_axis=0, concat_axis=1, tiled=True)  34.5 us
    dot_general x1, matrix products, accumulate(): return jnp.dot(left_part, right_part, preferred_element_type=jnp.float32)  21.2 us
    gather x2, local copies, waits for them, and re-layouts, on_device(): permuted = jnp.take(jnp.take(grid, virt_perm, axis=1), virt_perm, axis=3)  15.8 us
    reshape x2, local copies, waits for them, and re-layouts, on_device(): grid = cycle_term.reshape(row_count // V, V, out_cols // V, V)  14.2 us
    all_to_all x2, local copies, waits for them, and re-layouts, on_device(): lax.all_to_all(slab, ('row', 'col'), split_axis=1, concat_axis=0, tiled=T...  11.9 us
  transfers between devices with their start and end apart: 3, of which 3 were waited for; matrix products, arithmetic and copies ran while one was open for 2% of the time, Pallas kernels for 0%

commit v1 on v0

v1 whole, which is shorter than its diff:
```python
import functools

import jax
import jax.numpy as jnp
from jax import lax
from jax.experimental import pallas as pl
from jax.experimental.pallas import tpu as pltpu
from jax.sharding import PartitionSpec as P

V = 384
TILE = 768
MESH = pl.DeviceIdType.MESH


def place():
    r = lax.axis_index("row")
    c = lax.axis_index("col")
    return r // 2, r % 2, c // 4, (c // 2) % 2, c % 2


def device(z, xh, y, xl, k):
    return (lax.rem(z + 4, 4) * 2 + xh, lax.rem(y + 4, 4) * 4 + xl * 2 + k)


def gather_kernel(w_ref, t_ref, g_ref, eye_ref, comb_ref, comb_t_ref, wb, tb, acc, ssem, rsem, lsem):
    z, xh, y, xl, k = place()
    half = {"w": wb.shape[1] // 2, "t": tb.shape[1] // 2}
    depth = w_ref.shape[1]
    k_cols = pl.ds(pl.multiple_of(k * depth, 128), depth)

    up_y, down_y = device(z, xh, y + 1, xl, k), device(z, xh, y - 1, xl, k)
    up_z, down_z = device(z + 1, xh, y, xl, k), device(z - 1, xh, y, xl, k)
    over_lo = device(z, xh, y, 1 - xl, k)
    over_hi = device(z, 1 - xh, y, xl, k)
    sib = device(z, xh, y, xl, 1 - k)

    barrier = pltpu.get_barrier_semaphore()
    peers = (up_y, down_y, up_z, down_z, over_lo, over_hi, sib)
    for peer in peers:
        pl.semaphore_signal(barrier, inc=1, device_id=peer, device_id_type=MESH)

    def slot(along, which):
        return lax.rem(along + 4, 4) * 2 + which

    def w_at(dy, e, h):
        e_xl = xl if e == 0 else 1 - xl
        return wb.at[slot(y + dy, e_xl), pl.ds(h * half["w"], half["w"]), k_cols]

    def t_at(dz, e, h):
        e_xh = xh if e == 0 else 1 - xh
        return tb.at[slot(z + dz, e_xh), pl.ds(h * half["t"], half["t"]), :]

    copies = {}

    def send(name, ref, peer, src=None):
        i = len(copies)
        copies[name] = pltpu.make_async_remote_copy(
            src_ref=ref if src is None else src,
            dst_ref=ref,
            send_sem=ssem.at[i],
            recv_sem=rsem.at[i],
            device_id=peer,
            device_id_type=MESH,
        )
        copies[name].start()

    def got(name):
        copies[name].wait_recv()

    own_w = pltpu.make_async_copy(w_ref, wb.at[slot(y, xl), :, k_cols], lsem.at[0])
    own_t = pltpu.make_async_copy(t_ref, tb.at[slot(z, xh)], lsem.at[1])
    own_w.start()
    own_t.start()
    pl.semaphore_wait(barrier, len(peers))

    def w_src(h):
        return w_ref.at[pl.ds(h * half["w"], half["w"]), :]

    def t_src(h):
        return t_ref.at[pl.ds(h * half["t"], half["t"]), :]

    for first in (0, 1):
        a, b = first, 1 - first
        send(f"y+0{a}", w_at(0, 0, a), up_y, w_src(a))
        send(f"y-0{b}", w_at(0, 0, b), down_y, w_src(b))
        send(f"z+0{a}", t_at(0, 0, a), up_z, t_src(a))
        send(f"z-0{b}", t_at(0, 0, b), down_z, t_src(b))
        send(f"xl{a}", w_at(0, 0, a), over_lo, w_src(a))
        send(f"xh{a}", t_at(0, 0, a), over_hi, t_src(a))
        send(f"s0{a}", w_at(0, 0, a), sib, w_src(a))

    acc[...] = jnp.zeros_like(acc)

    def class_of(distance, other):
        near = lax.rem(distance + 8, 4)
        ring = jnp.where(near == 0, 1, jnp.where(near == 2, 3, 2))
        return jnp.where(other == 0, 1, ring)

    def multiply(stage):
        def block(q, carry):
            far = jnp.maximum(
                class_of(q // 2 - y, lax.rem(q % 2 + xl, 2)),
                class_of(q // 2 - z, lax.rem(q % 2 + xh, 2)),
            )

            @pl.when(far == stage)
            def _():
                rows = 512

                def tile(s, inner):
                    at = pl.ds(pl.multiple_of(s * rows, rows), rows)
                    acc[at, :] += jnp.dot(
                        wb[q, at, :], tb[q], preferred_element_type=jnp.float32
                    )
                    return inner

                lax.fori_loop(0, wb.shape[1] // rows, tile, 0)

            return carry

        lax.fori_loop(0, 8, block, 0)

    got("y+00")
    send("fy+0", w_at(-1, 0, 0), up_y)
    got("z+00")
    send("fz+0", t_at(-1, 0, 0), up_z)
    got("y-01")
    send("fy-0", w_at(1, 0, 1), down_y)
    got("z-01")
    send("fz-0", t_at(1, 0, 1), down_z)
    send("s-0", w_at(-1, 0, 0), sib)
    send("s+1", w_at(1, 0, 1), sib)
    for h in (0, 1):
        got(f"xl{h}")
        send(f"y+1{h}", w_at(0, 1, h), up_y)
        send(f"y-1{h}", w_at(0, 1, h), down_y)
        got(f"xh{h}")
        send(f"z+1{h}", t_at(0, 1, h), up_z)
        send(f"z-1{h}", t_at(0, 1, h), down_z)
        send(f"sx{h}", w_at(0, 1, h), sib)
        if h == 0:
            got("y+01")
            send("s-1", w_at(-1, 0, 1), sib)
            got("y-00")
            send("s+0", w_at(1, 0, 0), sib)
            got("z+01")
            got("z-00")
    got("fy+0")
    send("s20", w_at(2, 0, 0), sib)
    got("fy-0")
    send("s21", w_at(2, 0, 1), sib)
    got("fz+0")
    got("fz-0")
    own_w.wait()
    own_t.wait()
    got("y+10")
    send("fy+1", w_at(-1, 1, 0), up_y)
    got("z+10")
    send("fz+1", t_at(-1, 1, 0), up_z)
    send("sx-0", w_at(-1, 1, 0), sib)
    for name in ("s00", "s01", "s-0", "s-1", "s+0", "s+1", "sx0", "sx1", "s20", "s21"):
        got(name)
    multiply(1)
    got("y-11")
    send("fy-1", w_at(1, 1, 1), down_y)
    got("z-11")
    send("fz-1", t_at(1, 1, 1), down_z)
    send("sx+1", w_at(1, 1, 1), sib)
    got("y+11")
    send("sx-1", w_at(-1, 1, 1), sib)
    got("y-10")
    send("sx+0", w_at(1, 1, 0), sib)
    got("z+11")
    got("z-10")
    for name in ("sx-0", "sx-1", "sx+0", "sx+1"):
        got(name)
    multiply(2)
    got("fy+1")
    send("sx20", w_at(2, 1, 0), sib)
    got("fy-1")
    send("sx21", w_at(2, 1, 1), sib)
    got("fz+1")
    got("fz-1")
    got("sx20")
    got("sx21")
    multiply(3)

    select = g_ref[...]
    eye = eye_ref[...]
    for j in range(acc.shape[1] // V):
        cols = pl.ds(j * V, V)

        def block(i, carry, cols=cols):
            rows = pl.ds(pl.multiple_of(i * V, V), V)
            cyc = acc[rows, cols]
            hi = cyc.astype(jnp.bfloat16)
            lo = (cyc - hi.astype(jnp.float32)).astype(jnp.bfloat16)

            def exchanged(part):
                moved = jnp.dot(select, part, preferred_element_type=jnp.float32).astype(jnp.bfloat16)
                return lax.dot_general(
                    select, moved, (((1,), (1,)), ((), ())), preferred_element_type=jnp.float32
                )

            comb = (2.0 * cyc - (exchanged(hi) + exchanged(lo))).astype(jnp.bfloat16)
            comb_ref[rows, cols] = comb
            comb_t_ref[cols, rows] = lax.dot_general(
                eye, comb, (((1,), (1,)), ((), ())), preferred_element_type=jnp.float32
            ).astype(jnp.bfloat16)
            return carry

        lax.fori_loop(0, acc.shape[0] // V, block, 0)
    for copy in copies.values():
        copy.wait_send()


def on_device(interaction, cycle_amps, tile_mask, virt_perm, occ_energy, virt_energy, old_amps):
    row_count, depth = interaction.shape
    out_cols = cycle_amps.shape[1]
    row = lax.axis_index("row")
    col = lax.axis_index("col")
    row_tiles = row_count // TILE
    flags = lax.dynamic_slice(tile_mask, (row * row_tiles, (col * depth) // TILE), (row_tiles, 1))
    masked = (
        interaction.reshape(row_tiles, TILE, depth) * flags[:, :, None].astype(jnp.bfloat16)
    ).reshape(row_count, depth)
    lanes = jnp.arange(V, dtype=jnp.int32)
    select = (virt_perm[:, None] == lanes[None, :]).astype(jnp.bfloat16)
    eye = (lanes[:, None] == lanes[None, :]).astype(jnp.bfloat16)
    combined, combined_t = pl.pallas_call(
        gather_kernel,
        name="gather_multiply",
        out_shape=(
            jax.ShapeDtypeStruct((row_count, out_cols), jnp.bfloat16),
            jax.ShapeDtypeStruct((out_cols, row_count), jnp.bfloat16),
        ),
        in_specs=[pl.BlockSpec(memory_space=pl.ANY)] * 2 + [pl.BlockSpec(memory_space=pltpu.VMEM)] * 2,
        out_specs=(pl.BlockSpec(memory_space=pltpu.VMEM),) * 2,
        scratch_shapes=[
            pltpu.VMEM((8, row_count, 2 * depth), jnp.bfloat16),
            pltpu.VMEM((8, cycle_amps.shape[0], out_cols), jnp.bfloat16),
            pltpu.VMEM((row_count, out_cols), jnp.float32),
            pltpu.SemaphoreType.DMA((48,)),
            pltpu.SemaphoreType.DMA((48,)),
            pltpu.SemaphoreType.DMA((2,)),
        ],
        compiler_params=pltpu.CompilerParams(
            collective_id=1, has_side_effects=True, vmem_limit_bytes=60 * 1024 * 1024
        ),
    )(masked, cycle_amps, select, eye)
    slab = lax.all_to_all(combined, "col", split_axis=0, concat_axis=1, tiled=True)
    columns = lax.all_to_all(slab, ("row", "col"), split_axis=1, concat_axis=0, tiled=True)
    paired = slab.astype(jnp.float32) + columns.T.astype(jnp.float32)
    slab_rows = slab.shape[0]
    total_cols = slab.shape[1]
    slab_index = row * lax.axis_size("col") + col
    global_rows = slab_index * slab_rows + jnp.arange(slab_rows, dtype=jnp.int32)
    row_energy = virt_energy[global_rows % V] - occ_energy[global_rows // V]
    pair_energy = (virt_energy[None, :] - occ_energy[:, None]).reshape(total_cols)
    denominator = row_energy[:, None] + pair_energy[None, :]
    return old_amps.astype(jnp.float32) + paired / denominator


def solution(mesh):
    placed = (P("row", "col"), P("row", "col"), P(), P(), P(), P(), P(("row", "col"), None))
    return jax.shard_map(
        on_device, mesh=mesh, in_specs=placed, out_specs=P(("row", "col"), None), check_vma=False
    )
```

time: 425 us -> 231 us (0.54)
  waiting for transfers between devices: 253 us -> 34.2 us
  Pallas kernels: 0 us -> 107 us
  local copies, waits for them, and re-layouts: 63.8 us -> 26.2 us
  matrix products: 26.9 us -> 0 us
  between operations: 13.6 us -> 0.1 us
  other arithmetic: 22.4 us -> 17.9 us
    all_gather x2 -> x0, waiting for transfers between devices: 216 us -> none  [the longest x1 113 us: on_device(): amp_full = lax.all_gather(cycle_amps, 'row', axis=0, tiled=True)]
    pallas_call x0 -> x1, Pallas kernels: none -> 107 us  [on_device(): pl.pallas_call(gather_kernel, name='gather_multiply', out_shape=(jax.Shap...]
    dot_general x3 -> x0, matrix products: 26.9 us -> none  [the longest x1 21.2 us: accumulate(): return jnp.dot(left_part, right_part, preferred_element_type=jnp.float32)]
    reshape x2 -> x0, local copies, waits for them, and re-layouts: 14.2 us -> none  [on_device(): grid = cycle_term.reshape(row_count // V, V, out_cols // V, V)]
    gather x2, local copies, waits for them, and re-layouts: 15.8 us -> 2.49 us  [on_device(): row_energy = virt_energy[global_rows % V] - occ_energy[global_rows // V]]
    select_n x2 -> x0, local copies, waits for them, and re-layouts: 9.1 us -> none  [on_device(): permuted = jnp.take(jnp.take(grid, virt_perm, axis=1), virt_perm, axis=3)]
    select_n x6 -> x1, other arithmetic: 8.47 us -> 0.02 us  [on_device(): row_energy = virt_energy[global_rows % V] - occ_energy[global_rows // V]]
  transfers between devices with their start and end apart: 3 -> 1, of which waited for: 3 -> 1; matrix products, arithmetic and copies ran while one was open for 2% -> 3% of each run, Pallas kernels for 0% -> 0%
where the time goes in v1:
time: 231 us; the launch traced here: 229 us
  Pallas kernels  107 us (46%)
  blocking collectives  35.5 us (15%)
  waiting for transfers between devices  34.2 us (15%)
  local copies, waits for them, and re-layouts  26.2 us (11%)
  other arithmetic  17.9 us (8%)
  starting transfers between devices  7.71 us (3%)
    pallas_call x1, Pallas kernels, on_device(): pl.pallas_call(gather_kernel, name='gather_multiply', out_shape=(jax.Shap...  107 us
    all_to_all x1, blocking collectives, on_device(): lax.all_to_all(combined, 'col', split_axis=0, concat_axis=1, tiled=True)  35.5 us
    all_to_all x1, waiting for transfers between devices, on_device(): lax.all_to_all(slab, ('row', 'col'), split_axis=1, concat_axis=0, tiled=T...  34.2 us
    all_to_all x2, local copies, waits for them, and re-layouts, on_device(): lax.all_to_all(slab, ('row', 'col'), split_axis=1, concat_axis=0, tiled=T...  12 us
    convert_element_type x2, local copies, waits for them, and re-layouts, on_device(): paired = slab.astype(jnp.float32) + columns.T.astype(jnp.float32)  8.99 us
    all_to_all x1, starting transfers between devices, on_device(): lax.all_to_all(slab, ('row', 'col'), split_axis=1, concat_axis=0, tiled=T...  7.71 us
    add x1, other arithmetic, on_device(): return old_amps.astype(jnp.float32) + paired / denominator  6.97 us
    convert_element_type x1, other arithmetic, on_device(): paired = slab.astype(jnp.float32) + columns.T.astype(jnp.float32)  5.42 us
  transfers between devices with their start and end apart: 1, of which 1 were waited for; matrix products, arithmetic and copies ran while one was open for 3% of the time, Pallas kernels for 0%

profile of v1, /device:TPU:3, one launch (start us, length us, event | category | flops | bytes accessed | tf_op | source)
XLA Modules:
  0.0 228.5 jit_solution(9995052768513505978)
XLA Ops:
  0.0 0.8 convert_bitcast_fusion.1
  0.8 0.1 mul.27
  0.9 1.6 fusion.2
  2.5 2.6 %broadcast_multiply_fusion.w_ref = bf16[1536,384]{1,0:T(8,128)(2,1)} fusion(bf16[1536,384]{1,0:T(8,128)(2,1)} %param.7, bf16[1536]{0:T(1024)(128)(2,1)S(1)} %mul.28), kind=kLoop, calls=%fused_computation.8 | loop fusion | flops 589824 | bytes 2362368 | tf_op jit(solution)/shard_map/mul | solution.py:225
  5.1 106.8 %gather_multiply.1 = (bf16[1536,768]{1,0:T(8,128)(2,1)}, bf16[768,1536]{1,0:T(8,128)(2,1)}) custom-call(bf16[1536,384]{1,0:T(8,128)(2,1)} %broadcast_multiply_fusion.w_ref, bf16[768,768]{1,0:T(8,128)(2,1)} %t_ref.1, bf16[384,384]{1,0:T(8,128)(2,1)} %get-tuple-element.7.g_ref, bf16[384,384]{1,0:T(8,128)(2,1)} %get-tuple-element.8.eye_ref), custom_call_target="tpu_custom_call" | custom-call | tf_op jit(solution)/shard_map/gather_multiply/pallas_call | solution.py:230
  111.9 35.5 %all_to_all.29 = bf16[16,96,768]{2,1,0:T(8,128)(2,1)S(1)} all-to-all(bf16[16,96,768]{2,1,0:T(8,128)(2,1)} %bitcast.24), channel_id=1, replica_groups=mesh['row'=8,'col'=16] {'col'}, dimensions={0} | all-to-all | bytes 4718592 | tf_op jit(solution)/shard_map/all_to_all | solution.py:251
  147.3 2.7 %copy.12 = bf16[96,16,768]{2,1,0:T(8,128)(2,1)} copy(bf16[96,16,768]{2,0,1:T(8,128)(2,1)S(1)} %bitcast.22) | data formatting | bytes 4718592 | tf_op jit(solution)/shard_map/all_to_all | solution.py:251
  150.0 6.4 %all_to_all.25 = bf16[96,128,96]{2,1,0:T(8,128)(2,1)} reshape(bf16[96,16,768]{2,1,0:T(8,128)(2,1)} %copy.12) | data formatting | bytes 4718592 | tf_op jit(solution)/shard_map/all_to_all | solution.py:252
  156.4 5.6 %copy.13 = bf16[96,128,96]{2,0,1:T(8,128)(2,1)} copy(bf16[96,128,96]{2,1,0:T(8,128)(2,1)} %all_to_all.25) | data formatting | bytes 4718592 | tf_op jit(solution)/shard_map/all_to_all | solution.py:252
  162.0 0.0 copy-start.1
  162.0 0.0 copy-start
  162.0 7.7 %all-to-all-start.1 = ((bf16[96,128,96]{2,0,1:T(8,128)(2,1)}), bf16[96,128,96]{2,0,1:T(8,128)(2,1)}, u32[]{:S(2)}, u32[]{:S(2)}) async-start(bf16[96,128,96]{2,0,1:T(8,128)(2,1)} %copy.13), calls=%async_computation.1 | async-start | bytes 6291456 | tf_op jit(solution)/shard_map/all_to_all | solution.py:252
  169.8 0.0 copy-done.1
  169.8 1.3 gather_fusion
  171.0 0.0 copy-done
  171.1 1.2 gather_fusion.1
  172.3 0.1 broadcast_subtract_fusion
  172.4 0.5 convert_bitcast_fusion
  172.9 2.7 %copy.16 = f32[16,12,8,768]{3,2,0,1:T(8,128)} copy(f32[16,12,8,768]{3,2,1,0:T(8,128)S(1)} %convert_bitcast_fusion) | data formatting | bytes 9437184 | tf_op jit(solution)/shard_map/convert_element_type | solution.py:253
  175.5 34.2 %all-to-all-done.1 = bf16[96,128,96]{2,0,1:T(8,128)(2,1)} async-done(((bf16[96,128,96]{2,0,1:T(8,128)(2,1)}), bf16[96,128,96]{2,0,1:T(8,128)(2,1)}, u32[]{:S(2)}, u32[]{:S(2)}) %all-to-all-start.1) | async-done | bytes 2359328 | tf_op jit(solution)/shard_map/all_to_all | solution.py:252
  209.8 5.4 %convert_element_type.52 = f32[96,128,96]{2,0,1:T(8,128)} convert(bf16[96,128,96]{2,0,1:T(8,128)(2,1)} %all-to-all-done.1) | non-fusion elementwise | flops 1179648 | bytes 7077888 | tf_op jit(solution)/shard_map/convert_element_type | solution.py:253
  215.2 0.0 copy-start.2
  215.2 6.3 %copy.15 = f32[12288,96]{0,1:T(8,128)} copy(f32[12288,96]{1,0:T(8,128)} %bitcast.21) | data formatting | bytes 9437184 | tf_op jit(solution)/shard_map/convert_element_type | solution.py:253
  221.5 0.0 copy-done.2
  221.5 7.0 %fusion.1 = f32[96,12288]{1,0:T(8,128)} fusion(f32[96,12288]{1,0:T(8,128)} %bitcast.23, f32[12288,96]{0,1:T(8,128)} %copy.15, bf16[96,12288]{1,0:T(8,128)(2,1)S(1)} %copy-done.2, f32[12288]{0:T(1024)S(1)} %sub.43, f32[96]{0:T(128)S(1)} %sub.39), kind=kLoop, calls=%fused_computation.4 | loop fusion | flops 5898240 | bytes 16564608 | tf_op jit(solution)/shard_map/add | solution.py:261
  (6 shorter events, 0.1 us)
Async XLA Ops:
  162.0 7.8 %copy-start.1 = (f32[384]{0:T(512)S(1)}, f32[384]{0:T(512)}, u32[]{:S(2)}) copy-start(f32[384]{0:T(512)} %param.12) | copy-start | bytes 4612
  162.0 9.1 %copy-start = (f32[32]{0:T(128)S(1)}, f32[32]{0:T(128)}, u32[]{:S(2)}) copy-start(f32[32]{0:T(128)} %param.11) | copy-start | bytes 388
  162.0 47.8 %all-to-all-start.1 = ((bf16[96,128,96]{2,0,1:T(8,128)(2,1)}), bf16[96,128,96]{2,0,1:T(8,128)(2,1)}, u32[]{:S(2)}, u32[]{:S(2)}) async-start(bf16[96,128,96]{2,0,1:T(8,128)(2,1)} %copy.13), calls=%async_computation.1 | async-start | bytes 6291456 | tf_op jit(solution)/shard_map/all_to_all | solution.py:252
  215.2 6.3 %copy-start.2 = (bf16[96,12288]{1,0:T(8,128)(2,1)S(1)}, bf16[96,12288]{1,0:T(8,128)(2,1)}, u32[]{:S(2)}) copy-start(bf16[96,12288]{1,0:T(8,128)(2,1)} %param.13) | copy-start | bytes 7077892

commit v2 on v1

--- a/solution.py
+++ b/solution.py
@@ -22,10 +22,16 @@
     return (lax.rem(z + 4, 4) * 2 + xh, lax.rem(y + 4, 4) * 4 + xl * 2 + k)
 
 
-def gather_kernel(w_ref, t_ref, g_ref, eye_ref, comb_ref, comb_t_ref, wb, tb, acc, ssem, rsem, lsem):
+def cycle_kernel(
+    mask_ref, perm_ref, w_ref, t_ref,
+    rows_ref, cols_ref,
+    wb, tb, acc, comb, comb_t, pick, ssem, rsem, lsem, row_sems, col_sems, land_sems,
+):
+    row, col = lax.axis_index("row"), lax.axis_index("col")
     z, xh, y, xl, k = place()
     half = {"w": wb.shape[1] // 2, "t": tb.shape[1] // 2}
     depth = w_ref.shape[1]
+    tiles = acc.shape[0] // TILE
     k_cols = pl.ds(pl.multiple_of(k * depth, 128), depth)
 
     up_y, down_y = device(z, xh, y + 1, xl, k), device(z, xh, y - 1, xl, k)
@@ -35,9 +41,29 @@
     sib = device(z, xh, y, xl, 1 - k)
 
     barrier = pltpu.get_barrier_semaphore()
-    peers = (up_y, down_y, up_z, down_z, over_lo, over_hi, sib)
-    for peer in peers:
+
+    def greet(peer):
         pl.semaphore_signal(barrier, inc=1, device_id=peer, device_id_type=MESH)
+
+    for peer in (up_z, down_z, over_hi):
+        greet(peer)
+
+    def greet_row(step, carry):
+        greet((row, lax.rem(col + step, 16)))
+        return carry
+
+    lax.fori_loop(1, 16, greet_row, 0)
+    col_source = 2 * row + col // 8
+
+    def greet_source(step, carry):
+        @pl.when(jnp.logical_or(step != row, col_source != col))
+        def _():
+            greet((step, col_source))
+
+        return carry
+
+    lax.fori_loop(0, 8, greet_source, 0)
+    expected = 3 + 15 + 8 - jnp.where(col_source == col, 1, 0)
 
     def slot(along, which):
         return lax.rem(along + 4, 4) * 2 + which
@@ -71,7 +97,7 @@
     own_t = pltpu.make_async_copy(t_ref, tb.at[slot(z, xh)], lsem.at[1])
     own_w.start()
     own_t.start()
-    pl.semaphore_wait(barrier, len(peers))
+    pl.semaphore_wait(barrier, expected)
 
     def w_src(h):
         return w_ref.at[pl.ds(h * half["w"], half["w"]), :]
@@ -90,6 +116,8 @@
         send(f"s0{a}", w_at(0, 0, a), sib, w_src(a))
 
     acc[...] = jnp.zeros_like(acc)
+    orbital = lax.broadcasted_iota(jnp.int32, pick.shape, 0)
+    pick[...] = jnp.where(orbital == perm_ref[...], 1.0, 0.0).T.astype(jnp.bfloat16)
 
     def class_of(distance, other):
         near = lax.rem(distance + 8, 4)
@@ -105,16 +133,15 @@
 
             @pl.when(far == stage)
             def _():
-                rows = 512
-
-                def tile(s, inner):
-                    at = pl.ds(pl.multiple_of(s * rows, rows), rows)
-                    acc[at, :] += jnp.dot(
+                def tile(p, inner):
+                    at = pl.ds(pl.multiple_of(p * TILE, TILE), TILE)
+                    kept = mask_ref[row * tiles + p, q].astype(jnp.float32)
+                    acc[at, :] += kept * jnp.dot(
                         wb[q, at, :], tb[q], preferred_element_type=jnp.float32
                     )
                     return inner
 
-                lax.fori_loop(0, wb.shape[1] // rows, tile, 0)
+                lax.fori_loop(0, tiles, tile, 0)
 
             return carry
 
@@ -185,33 +212,95 @@
     got("sx21")
     multiply(3)
 
-    select = g_ref[...]
-    eye = eye_ref[...]
-    for j in range(acc.shape[1] // V):
-        cols = pl.ds(j * V, V)
-
-        def block(i, carry, cols=cols):
-            rows = pl.ds(pl.multiple_of(i * V, V), V)
-            cyc = acc[rows, cols]
-            hi = cyc.astype(jnp.bfloat16)
-            lo = (cyc - hi.astype(jnp.float32)).astype(jnp.bfloat16)
-
-            def exchanged(part):
-                moved = jnp.dot(select, part, preferred_element_type=jnp.float32).astype(jnp.bfloat16)
-                return lax.dot_general(
-                    select, moved, (((1,), (1,)), ((), ())), preferred_element_type=jnp.float32
-                )
-
-            comb = (2.0 * cyc - (exchanged(hi) + exchanged(lo))).astype(jnp.bfloat16)
-            comb_ref[rows, cols] = comb
-            comb_t_ref[cols, rows] = lax.dot_general(
-                eye, comb, (((1,), (1,)), ((), ())), preferred_element_type=jnp.float32
-            ).astype(jnp.bfloat16)
+    part = V // 4
+    me = row * 16 + col
+    row_base = row * acc.shape[0]
+    col_base = col * acc.shape[1]
+
+    def block_at(t):
+        return lax.rem(y + t // 2, 4), lax.rem(t, 2)
+
+    def exchange(t):
+        i, j = block_at(t)
+        rows = pl.ds(pl.multiple_of(i * V, V), V)
+        cols = pl.ds(pl.multiple_of(j * V, V), V)
+        select = pick[...]
+        cyc = acc[rows, cols]
+        hi = cyc.astype(jnp.bfloat16)
+        lo = (cyc - hi.astype(jnp.float32)).astype(jnp.bfloat16)
+
+        def exchanged(piece):
+            moved = jnp.dot(select, piece, preferred_element_type=jnp.float32).astype(jnp.bfloat16)
+            return lax.dot_general(
+                select, moved, (((1,), (1,)), ((), ())), preferred_element_type=jnp.float32
+            )
+
+        combined = (2.0 * cyc - (exchanged(hi) + exchanged(lo))).astype(jnp.bfloat16)
+        comb[rows, cols] = combined
+        comb_t[cols, rows] = combined.T
+
+    def pieces(t, s):
+        i, j = block_at(t)
+        n = t * 4 + s
+        row_src = comb.at[
+            pl.ds(pl.multiple_of(i * V + s * part, part), part), pl.ds(pl.multiple_of(j * V, V), V)
+        ]
+        row_dst = rows_ref.at[:, pl.ds(pl.multiple_of(col_base + j * V, V), V)]
+        col_src = comb_t.at[
+            pl.ds(pl.multiple_of(j * V + s * part, part), part), pl.ds(pl.multiple_of(i * V, V), V)
+        ]
+        col_dst = cols_ref.at[:, pl.ds(pl.multiple_of(row_base + i * V, V), V)]
+        return (
+            (row_src, row_dst, row_sems.at[n], land_sems.at[0], row, i * 4 + s),
+            (col_src, col_dst, col_sems.at[n], land_sems.at[1], col // 2, lax.rem(col, 2) * 8 + j * 4 + s),
+        )
+
+    def each_piece(t, remote_step, local_step):
+        def piece(s, carry):
+            for src, dst, sent, landed, to_row, to_col in pieces(t, s):
+                here = to_row * 16 + to_col == me
+
+                @pl.when(here)
+                def _():
+                    local_step(pltpu.make_async_copy(src, dst, landed))
+
+                @pl.when(jnp.logical_not(here))
+                def _():
+                    remote_step(
+                        pltpu.make_async_remote_copy(
+                            src_ref=src, dst_ref=dst, send_sem=sent, recv_sem=landed,
+                            device_id=(to_row, to_col), device_id_type=MESH,
+                        )
+                    )
+
             return carry
 
-        lax.fori_loop(0, acc.shape[0] // V, block, 0)
+        lax.fori_loop(0, 4, piece, 0)
+
+    def start(t):
+        each_piece(t, lambda copy: copy.start(), lambda copy: copy.start())
+
+    def step(t, carry):
+        exchange(t)
+
+        @pl.when(t > 0)
+        def _():
+            start(t - 1)
+
+        return carry
+
+    lax.fori_loop(0, 8, step, 0)
+    start(7)
     for copy in copies.values():
         copy.wait_send()
+
+    def sent(t, carry):
+        each_piece(t, lambda copy: copy.wait_send(), lambda copy: None)
+        return carry
+
+    lax.fori_loop(0, 8, sent, 0)
+    pltpu.make_async_copy(rows_ref, rows_ref, land_sems.at[0]).wait()
+    pltpu.make_async_copy(cols_ref, cols_ref, land_sems.at[1]).wait()
 
 
 def on_device(interaction, cycle_amps, tile_mask, virt_perm, occ_energy, virt_energy, old_amps):
@@ -219,43 +308,43 @@
     out_cols = cycle_amps.shape[1]
     row = lax.axis_index("row")
     col = lax.axis_index("col")
-    row_tiles = row_count // TILE
-    flags = lax.dynamic_slice(tile_mask, (row * row_tiles, (col * depth) // TILE), (row_tiles, 1))
-    masked = (
-        interaction.reshape(row_tiles, TILE, depth) * flags[:, :, None].astype(jnp.bfloat16)
-    ).reshape(row_count, depth)
-    lanes = jnp.arange(V, dtype=jnp.int32)
-    select = (virt_perm[:, None] == lanes[None, :]).astype(jnp.bfloat16)
-    eye = (lanes[:, None] == lanes[None, :]).astype(jnp.bfloat16)
-    combined, combined_t = pl.pallas_call(
-        gather_kernel,
-        name="gather_multiply",
-        out_shape=(
-            jax.ShapeDtypeStruct((row_count, out_cols), jnp.bfloat16),
-            jax.ShapeDtypeStruct((out_cols, row_count), jnp.bfloat16),
-        ),
-        in_specs=[pl.BlockSpec(memory_space=pl.ANY)] * 2 + [pl.BlockSpec(memory_space=pltpu.VMEM)] * 2,
-        out_specs=(pl.BlockSpec(memory_space=pltpu.VMEM),) * 2,
+    total_cols = old_amps.shape[1]
+    slab_rows = old_amps.shape[0]
+    slab, columns = pl.pallas_call(
+        cycle_kernel,
+        name="cycle",
+        out_shape=(jax.ShapeDtypeStruct((slab_rows, total_cols), jnp.bfloat16),) * 2,
+        in_specs=[
+            pl.BlockSpec(memory_space=pltpu.SMEM),
+            pl.BlockSpec(memory_space=pltpu.VMEM),
+            pl.BlockSpec(memory_space=pl.ANY),
+            pl.BlockSpec(memory_space=pl.ANY),
+        ],
+        out_specs=(pl.BlockSpec(memory_space=pl.ANY),) * 2,
         scratch_shapes=[
             pltpu.VMEM((8, row_count, 2 * depth), jnp.bfloat16),
             pltpu.VMEM((8, cycle_amps.shape[0], out_cols), jnp.bfloat16),
             pltpu.VMEM((row_count, out_cols), jnp.float32),
+            pltpu.VMEM((row_count, out_cols), jnp.bfloat16),
+            pltpu.VMEM((out_cols, row_count), jnp.bfloat16),
+            pltpu.VMEM((V, V), jnp.bfloat16),
             pltpu.SemaphoreType.DMA((48,)),
             pltpu.SemaphoreType.DMA((48,)),
+            pltpu.SemaphoreType.DMA((2,)),
+            pltpu.SemaphoreType.DMA((32,)),
+            pltpu.SemaphoreType.DMA((32,)),
             pltpu.SemaphoreType.DMA((2,)),
         ],
         compiler_params=pltpu.CompilerParams(
             collective_id=1, has_side_effects=True, vmem_limit_bytes=60 * 1024 * 1024
         ),
-    )(masked, cycle_amps, select, eye)
-    slab = lax.all_to_all(combined, "col", split_axis=0, concat_axis=1, tiled=True)
-    columns = lax.all_to_all(slab, ("row", "col"), split_axis=1, concat_axis=0, tiled=True)
-    paired = slab.astype(jnp.float32) + columns.T.astype(jnp.float32)
-    slab_rows = slab.shape[0]
-    total_cols = slab.shape[1]
+    )(tile_mask, virt_perm.reshape(1, V), interaction, cycle_amps)
+    paired = slab.astype(jnp.float32) + columns.astype(jnp.float32)
     slab_index = row * lax.axis_size("col") + col
-    global_rows = slab_index * slab_rows + jnp.arange(slab_rows, dtype=jnp.int32)
-    row_energy = virt_energy[global_rows % V] - occ_energy[global_rows // V]
+    per_orbital = V // slab_rows
+    row_energy = lax.dynamic_slice(
+        virt_energy, (slab_index % per_orbital * slab_rows,), (slab_rows,)
+    ) - lax.dynamic_slice(occ_energy, (slab_index // per_orbital,), (1,))
     pair_energy = (virt_energy[None, :] - occ_energy[:, None]).reshape(total_cols)
     denominator = row_energy[:, None] + pair_energy[None, :]
     return old_amps.astype(jnp.float32) + paired / denominator

time: 231 us -> 171 us (0.74)
  Pallas kernels: 107 us -> 156 us
  blocking collectives: 35.5 us -> 0 us
  waiting for transfers between devices: 34.2 us -> 0 us
  local copies, waits for them, and re-layouts: 26.2 us -> 3.86 us
  other arithmetic: 17.9 us -> 8.71 us
  starting transfers between devices: 7.71 us -> 0 us
    pallas_call x1, Pallas kernels: 107 us -> 156 us  [on_device(): pl.pallas_call(cycle_kernel, name='cycle', out_shape=(jax.ShapeDtypeStruc...]
    all_to_all x1 -> x0, blocking collectives: 35.5 us -> none  [on_device(): lax.all_to_all(combined, 'col', split_axis=0, concat_axis=1, tiled=True)]
    all_to_all x1 -> x0, waiting for transfers between devices: 34.2 us -> none  [on_device(): lax.all_to_all(slab, ('row', 'col'), split_axis=1, concat_axis=0, tiled=T...]
    all_to_all x3 -> x0, local copies, waits for them, and re-layouts: 14.7 us -> none  [the longest x2 12 us: on_device(): lax.all_to_all(slab, ('row', 'col'), split_axis=1, concat_axis=0, tiled=T...]
    convert_element_type x2 -> x0, local copies, waits for them, and re-layouts: 8.99 us -> none  [on_device(): paired = slab.astype(jnp.float32) + columns.T.astype(jnp.float32)]
    convert_element_type x3 -> x0, other arithmetic: 7.82 us -> none  [the longest x1 5.42 us: on_device(): paired = slab.astype(jnp.float32) + columns.T.astype(jnp.float32)]
    all_to_all x1 -> x0, starting transfers between devices: 7.71 us -> none  [on_device(): lax.all_to_all(slab, ('row', 'col'), split_axis=1, concat_axis=0, tiled=T...]
    mul x1 -> x0, other arithmetic: 2.56 us -> none  [on_device(): interaction.reshape(row_tiles, TILE, depth)]
  transfers between devices with their start and end apart: 1 -> 0, of which waited for: 1 -> 0; matrix products, arithmetic and copies ran while one was open for 3% -> 0% of each run, Pallas kernels for 0% -> 0%
where the time goes in v2:
time: 171 us; the launch traced here: 169 us
  Pallas kernels  156 us (91%)
  other arithmetic  8.71 us (5%)
  local copies, waits for them, and re-layouts  3.86 us (2%)
    pallas_call x1, Pallas kernels, on_device(): pl.pallas_call(cycle_kernel, name='cycle', out_shape=(jax.ShapeDtypeStruc...  156 us
    add x1, other arithmetic, on_device(): return old_amps.astype(jnp.float32) + paired / denominator  6.54 us

profile of v2, /device:TPU:3, one launch (start us, length us, event | category | flops | bytes accessed | tf_op | source)
XLA Modules:
  0.0 168.7 jit_solution(6986266233099935703)
XLA Ops:
  0.0 1.2 dynamic_slice.7
  1.2 1.4 dynamic-slice_subtract_fusion
  2.6 1.3 reshape.20.perm_ref
  3.9 1.4 copy.8.mask_ref
  5.3 0.8 broadcast_subtract_fusion
  6.0 156.1 %cycle.1 = (bf16[96,12288]{1,0:T(8,128)(2,1)}, bf16[96,12288]{1,0:T(8,128)(2,1)}) custom-call(s32[16,8]{1,0:T(8,128)} %copy.8.mask_ref, s32[1,384]{1,0:T(1,128)} %reshape.20.perm_ref, bf16[1536,384]{1,0:T(8,128)(2,1)} %w_ref.1, bf16[768,768]{1,0:T(8,128)(2,1)} %t_ref.1), custom_call_target="tpu_custom_call" | custom-call | tf_op jit(solution)/shard_map/cycle/pallas_call | solution.py:313
  162.2 6.5 %divide_add_fusion = f32[96,12288]{1,0:T(8,128)} fusion(bf16[96,12288]{1,0:T(8,128)(2,1)} %get-tuple-element.8, bf16[96,12288]{1,0:T(8,128)(2,1)} %get-tuple-element.7, bf16[96,12288]{1,0:T(8,128)(2,1)} %param.13, f32[12288]{0:T(1024)S(1)} %sub.41, f32[96]{0:T(128)S(1)} %dynamic-slice_subtract_fusion), kind=kLoop, calls=%fused_computation | loop fusion | flops 8257536 | bytes 11846016 | tf_op jit(solution)/shard_map/add | solution.py:350
  (1 shorter events, 0.0 us)

commit v3 on v2

--- a/solution.py
+++ b/solution.py
@@ -25,7 +25,7 @@
 def cycle_kernel(
     mask_ref, perm_ref, w_ref, t_ref,
     rows_ref, cols_ref,
-    wb, tb, acc, comb, comb_t, pick, ssem, rsem, lsem, row_sems, col_sems, land_sems,
+    wb, tb, acc, comb, comb_t, pick, mask, perm, ssem, rsem, lsem, row_sems, col_sems, land_sems,
 ):
     row, col = lax.axis_index("row"), lax.axis_index("col")
     z, xh, y, xl, k = place()
@@ -95,8 +95,12 @@
 
     own_w = pltpu.make_async_copy(w_ref, wb.at[slot(y, xl), :, k_cols], lsem.at[0])
     own_t = pltpu.make_async_copy(t_ref, tb.at[slot(z, xh)], lsem.at[1])
-    own_w.start()
-    own_t.start()
+    small = (
+        pltpu.make_async_copy(mask_ref, mask, lsem.at[2]),
+        pltpu.make_async_copy(perm_ref, perm, lsem.at[3]),
+    )
+    for copy in (*small, own_w, own_t):
+        copy.start()
     pl.semaphore_wait(barrier, expected)
 
     def w_src(h):
@@ -116,8 +120,10 @@
         send(f"s0{a}", w_at(0, 0, a), sib, w_src(a))
 
     acc[...] = jnp.zeros_like(acc)
+    for copy in small:
+        copy.wait()
     orbital = lax.broadcasted_iota(jnp.int32, pick.shape, 0)
-    pick[...] = jnp.where(orbital == perm_ref[...], 1.0, 0.0).T.astype(jnp.bfloat16)
+    pick[...] = jnp.where(orbital == perm[...].reshape(1, V), 1.0, 0.0).T.astype(jnp.bfloat16)
 
     def class_of(distance, other):
         near = lax.rem(distance + 8, 4)
@@ -135,7 +141,7 @@
             def _():
                 def tile(p, inner):
                     at = pl.ds(pl.multiple_of(p * TILE, TILE), TILE)
-                    kept = mask_ref[row * tiles + p, q].astype(jnp.float32)
+                    kept = mask[q, row * tiles + p].astype(jnp.float32)
                     acc[at, :] += kept * jnp.dot(
                         wb[q, at, :], tb[q], preferred_element_type=jnp.float32
                     )
@@ -218,7 +224,9 @@
     col_base = col * acc.shape[1]
 
     def block_at(t):
-        return lax.rem(y + t // 2, 4), lax.rem(t, 2)
+        n = t // 2
+        hop = jnp.where(n == 0, 1, jnp.where(n == 1, 3, jnp.where(n == 2, 2, 0)))
+        return lax.rem(y + jnp.where(k == 0, hop, 4 - hop), 4), lax.rem(t + 1 + y, 2)
 
     def exchange(t):
         i, j = block_at(t)
@@ -303,23 +311,68 @@
     pltpu.make_async_copy(cols_ref, cols_ref, land_sems.at[1]).wait()
 
 
+def update_kernel(
+    rows_ref, cols_ref, old_ref, virt_ref, occ_ref, out_ref, old, out, virt, occ, in_sems, out_sems
+):
+    slab_rows = old.shape[0]
+    chunks = in_sems.shape[0] - 2
+    width = old.shape[1] // chunks
+    slab = lax.axis_index("row") * 16 + lax.axis_index("col")
+    small = (
+        pltpu.make_async_copy(virt_ref, virt, in_sems.at[chunks]),
+        pltpu.make_async_copy(occ_ref, occ, in_sems.at[chunks + 1]),
+    )
+    for copy in small:
+        copy.start()
+
+    def chunk_of(n):
+        return (slice(None), pl.ds(n * width, width))
+
+    reads = [
+        pltpu.make_async_copy(old_ref.at[chunk_of(n)], old.at[chunk_of(n)], in_sems.at[n])
+        for n in range(chunks)
+    ]
+    writes = [
+        pltpu.make_async_copy(out.at[chunk_of(n)], out_ref.at[chunk_of(n)], out_sems.at[n])
+        for n in range(chunks)
+    ]
+    for copy in reads:
+        copy.start()
+    for copy in small:
+        copy.wait()
+    per_orbital = V // slab_rows
+    virtual = virt[...].reshape(1, V)
+    lanes = lax.broadcasted_iota(jnp.int32, (slab_rows, V), 1)
+    wanted = lax.broadcasted_iota(jnp.int32, (slab_rows, V), 0) + lax.rem(slab, per_orbital) * slab_rows
+    row_energy = (
+        jnp.sum(jnp.where(lanes == wanted, virtual, 0.0), axis=1, keepdims=True)
+        - occ[slab // per_orbital]
+    )
+    for n in range(chunks):
+        reads[n].wait()
+
+        def orbital(j, carry):
+            cols = pl.ds(pl.multiple_of(j * V, V), V)
+            denominator = row_energy + (virtual - occ[j])
+            paired = rows_ref[:, cols].astype(jnp.float32) + cols_ref[:, cols].astype(jnp.float32)
+            out[:, cols] = old[:, cols].astype(jnp.float32) + paired / denominator
+            return carry
+
+        lax.fori_loop(n * (width // V), (n + 1) * (width // V), orbital, 0)
+        writes[n].start()
+    for copy in writes:
+        copy.wait()
+
+
 def on_device(interaction, cycle_amps, tile_mask, virt_perm, occ_energy, virt_energy, old_amps):
     row_count, depth = interaction.shape
     out_cols = cycle_amps.shape[1]
-    row = lax.axis_index("row")
-    col = lax.axis_index("col")
-    total_cols = old_amps.shape[1]
-    slab_rows = old_amps.shape[0]
-    slab, columns = pl.pallas_call(
+    slab_rows, total_cols = old_amps.shape
+    rows, cols = pl.pallas_call(
         cycle_kernel,
         name="cycle",
         out_shape=(jax.ShapeDtypeStruct((slab_rows, total_cols), jnp.bfloat16),) * 2,
-        in_specs=[
-            pl.BlockSpec(memory_space=pltpu.SMEM),
-            pl.BlockSpec(memory_space=pltpu.VMEM),
-            pl.BlockSpec(memory_space=pl.ANY),
-            pl.BlockSpec(memory_space=pl.ANY),
-        ],
+        in_specs=[pl.BlockSpec(memory_space=pltpu.HBM)] * 4,
         out_specs=(pl.BlockSpec(memory_space=pl.ANY),) * 2,
         scratch_shapes=[
             pltpu.VMEM((8, row_count, 2 * depth), jnp.bfloat16),
@@ -328,26 +381,41 @@
             pltpu.VMEM((row_count, out_cols), jnp.bfloat16),
             pltpu.VMEM((out_cols, row_count), jnp.bfloat16),
             pltpu.VMEM((V, V), jnp.bfloat16),
+            pltpu.SMEM(tile_mask.shape[::-1], jnp.int32),
+            pltpu.VMEM((V,), jnp.int32),
             pltpu.SemaphoreType.DMA((48,)),
             pltpu.SemaphoreType.DMA((48,)),
-            pltpu.SemaphoreType.DMA((2,)),
+            pltpu.SemaphoreType.DMA((4,)),
             pltpu.SemaphoreType.DMA((32,)),
             pltpu.SemaphoreType.DMA((32,)),
             pltpu.SemaphoreType.DMA((2,)),
         ],
         compiler_params=pltpu.CompilerParams(
-            collective_id=1, has_side_effects=True, vmem_limit_bytes=60 * 1024 * 1024
+            collective_id=1, has_side_effects=True, vmem_limit_bytes=44 * 1024 * 1024
         ),
-    )(tile_mask, virt_perm.reshape(1, V), interaction, cycle_amps)
-    paired = slab.astype(jnp.float32) + columns.astype(jnp.float32)
-    slab_index = row * lax.axis_size("col") + col
-    per_orbital = V // slab_rows
-    row_energy = lax.dynamic_slice(
-        virt_energy, (slab_index % per_orbital * slab_rows,), (slab_rows,)
-    ) - lax.dynamic_slice(occ_energy, (slab_index // per_orbital,), (1,))
-    pair_energy = (virt_energy[None, :] - occ_energy[:, None]).reshape(total_cols)
-    denominator = row_energy[:, None] + pair_energy[None, :]
-    return old_amps.astype(jnp.float32) + paired / denominator
+    )(
+        *(
+            pltpu.with_memory_space_constraint(operand, pltpu.HBM)
+            for operand in (tile_mask.T, virt_perm, interaction, cycle_amps)
+        )
+    )
+    chunks = 4
+    return pl.pallas_call(
+        update_kernel,
+        name="update",
+        out_shape=jax.ShapeDtypeStruct((slab_rows, total_cols), jnp.float32),
+        in_specs=[pl.BlockSpec(memory_space=pltpu.VMEM)] * 2 + [pl.BlockSpec(memory_space=pltpu.HBM)] * 3,
+        out_specs=pl.BlockSpec(memory_space=pltpu.HBM),
+        scratch_shapes=[
+            pltpu.VMEM((slab_rows, total_cols), jnp.bfloat16),
+            pltpu.VMEM((slab_rows, total_cols), jnp.float32),
+            pltpu.VMEM((V,), jnp.float32),
+            pltpu.SMEM((occ_energy.shape[0],), jnp.float32),
+            pltpu.SemaphoreType.DMA((chunks + 2,)),
+            pltpu.SemaphoreType.DMA((chunks,)),
+        ],
+        compiler_params=pltpu.CompilerParams(vmem_limit_bytes=12 * 1024 * 1024),
+    )(rows, cols, old_amps, virt_energy, occ_energy)
 
 
 def solution(mesh):

time: 171 us -> 157 us (0.918)
  other arithmetic: 8.71 us -> 0 us
  local copies, waits for them, and re-layouts: 3.86 us -> 0.01 us
    add x1 -> x0, other arithmetic: 6.54 us -> none  [on_device(): return old_amps.astype(jnp.float32) + paired / denominator]
    pallas_call x0 -> x1, Pallas kernels: none -> 3.28 us  [on_device(): pl.pallas_call(update_kernel, name='update', out_shape=jax.ShapeDtypeStru...]
    pallas_call x1, Pallas kernels: 156 us -> 153 us  [on_device(): pl.pallas_call(cycle_kernel, name='cycle', out_shape=(jax.ShapeDtypeStruc...]
    sub x2 -> x0, other arithmetic: 2.17 us -> none  [the longest x1 1.4 us: on_device(): lax.dynamic_slice(virt_energy, (slab_index % per_orbital * slab_rows,), (...]
where the time goes in v3:
time: 157 us; the launch traced here: 156 us
  Pallas kernels  156 us (99%)
    pallas_call x1, Pallas kernels, on_device(): pl.pallas_call(cycle_kernel, name='cycle', out_shape=(jax.ShapeDtypeStruc...  153 us
    pallas_call x1, Pallas kernels, on_device(): pl.pallas_call(update_kernel, name='update', out_shape=jax.ShapeDtypeStru...  3.28 us

profile of v3, /device:TPU:3, one launch (start us, length us, event | category | flops | bytes accessed | tf_op | source)
XLA Modules:
  0.0 156.4 jit_solution(17136615519894768005)
XLA Ops:
  0.0 0.0 copy-start
  0.0 0.0 copy-start.1
  0.0 0.0 copy-start.2
  0.0 153.1 %cycle.1 = (bf16[96,12288]{1,0:T(8,128)(2,1)S(1)}, bf16[96,12288]{1,0:T(8,128)(2,1)S(1)}) custom-call(s32[8,16]{1,0:T(8,128)} %bitcast.1, s32[384]{0:T(512)} %perm_ref.1, bf16[1536,384]{1,0:T(8,128)(2,1)} %w_ref.1, bf16[768,768]{1,0:T(8,128)(2,1)} %t_ref.1), custom_call_target="tpu_custom_call" | custom-call | tf_op jit(solution)/shard_map/cycle/pallas_call | solution.py:371
  153.1 0.0 copy-done
  153.1 0.0 copy-done.1
  153.1 0.0 copy-done.2
  153.1 3.3 %update.1 = f32[96,12288]{1,0:T(8,128)} custom-call(bf16[96,12288]{1,0:T(8,128)(2,1)S(1)} %get-tuple-element.7.rows_ref, bf16[96,12288]{1,0:T(8,128)(2,1)S(1)} %get-tuple-element.8.cols_ref, bf16[96,12288]{1,0:T(8,128)(2,1)S(1)} %copy-done, f32[384]{0:T(512)S(1)} %copy-done.1, f32[32]{0:T(128)S(1)} %copy-done.2), custom_call_target="tpu_custom_call" | custom-call | tf_op jit(solution)/shard_map/update/pallas_call | solution.py:403
Async XLA Ops:
  0.0 153.1 %copy-start = (bf16[96,12288]{1,0:T(8,128)(2,1)S(1)}, bf16[96,12288]{1,0:T(8,128)(2,1)}, u32[]{:S(2)}) copy-start(bf16[96,12288]{1,0:T(8,128)(2,1)} %old_ref.1) | copy-start | bytes 7077892
  0.0 153.1 %copy-start.1 = (f32[384]{0:T(512)S(1)}, f32[384]{0:T(512)}, u32[]{:S(2)}) copy-start(f32[384]{0:T(512)} %virt_ref.1) | copy-start | bytes 4612
  0.0 153.1 %copy-start.2 = (f32[32]{0:T(128)S(1)}, f32[32]{0:T(128)}, u32[]{:S(2)}) copy-start(f32[32]{0:T(128)} %occ_ref.1) | copy-start | bytes 388

commit v4 on v3

--- a/solution.py
+++ b/solution.py
@@ -29,9 +29,8 @@
 ):
     row, col = lax.axis_index("row"), lax.axis_index("col")
     z, xh, y, xl, k = place()
-    half = {"w": wb.shape[1] // 2, "t": tb.shape[1] // 2}
     depth = w_ref.shape[1]
-    tiles = acc.shape[0] // TILE
+    tiles = comb.shape[0] // TILE
     k_cols = pl.ds(pl.multiple_of(k * depth, 128), depth)
 
     up_y, down_y = device(z, xh, y + 1, xl, k), device(z, xh, y - 1, xl, k)
@@ -68,13 +67,17 @@
     def slot(along, which):
         return lax.rem(along + 4, 4) * 2 + which
 
-    def w_at(dy, e, h):
-        e_xl = xl if e == 0 else 1 - xl
-        return wb.at[slot(y + dy, e_xl), pl.ds(h * half["w"], half["w"]), k_cols]
-
-    def t_at(dz, e, h):
-        e_xh = xh if e == 0 else 1 - xh
-        return tb.at[slot(z + dz, e_xh), pl.ds(h * half["t"], half["t"]), :]
+    first = lax.rem(1 + y, 2)
+    second = 1 - first
+
+    def w_at(dy, e, rows):
+        return wb.at[slot(y + dy, xl if e == 0 else 1 - xl), pl.ds(*rows), k_cols]
+
+    def t_part(j, rows):
+        return pl.ds(*rows), pl.ds(pl.multiple_of((second if j else first) * V, V), V)
+
+    def t_at(dz, e, j, rows):
+        return tb.at[(slot(z + dz, xh if e == 0 else 1 - xh), *t_part(j, rows))]
 
     copies = {}
 
@@ -90,150 +93,102 @@
         )
         copies[name].start()
 
-    def got(name):
-        copies[name].wait_recv()
-
-    own_w = pltpu.make_async_copy(w_ref, wb.at[slot(y, xl), :, k_cols], lsem.at[0])
-    own_t = pltpu.make_async_copy(t_ref, tb.at[slot(z, xh)], lsem.at[1])
+    def got(*names):
+        for name in names:
+            copies[name].wait_recv()
+
+    def w_own(name, peer, rows):
+        send(name, w_at(0, 0, rows), peer, w_ref.at[pl.ds(*rows), :])
+
+    def t_own(name, j, peer, rows):
+        send(name, t_at(0, 0, j, rows), peer, t_ref.at[t_part(j, rows)])
+
+    half = wb.shape[1] // 2
+    w_a, w_b = (0, half), (half, half)
+    w_up, w_mid, w_down = (0, V), (V, 2 * V), (3 * V, V)
+    t_all, t_a, t_b = (0, 2 * V), (0, V), (V, V)
+
     small = (
         pltpu.make_async_copy(mask_ref, mask, lsem.at[2]),
         pltpu.make_async_copy(perm_ref, perm, lsem.at[3]),
     )
-    for copy in (*small, own_w, own_t):
+    own = (
+        pltpu.make_async_copy(w_ref, wb.at[slot(y, xl), :, k_cols], lsem.at[0]),
+        pltpu.make_async_copy(t_ref, tb.at[slot(z, xh)], lsem.at[1]),
+    )
+    for copy in small + own:
         copy.start()
     pl.semaphore_wait(barrier, expected)
 
-    def w_src(h):
-        return w_ref.at[pl.ds(h * half["w"], half["w"]), :]
-
-    def t_src(h):
-        return t_ref.at[pl.ds(h * half["t"], half["t"]), :]
-
-    for first in (0, 1):
-        a, b = first, 1 - first
-        send(f"y+0{a}", w_at(0, 0, a), up_y, w_src(a))
-        send(f"y-0{b}", w_at(0, 0, b), down_y, w_src(b))
-        send(f"z+0{a}", t_at(0, 0, a), up_z, t_src(a))
-        send(f"z-0{b}", t_at(0, 0, b), down_z, t_src(b))
-        send(f"xl{a}", w_at(0, 0, a), over_lo, w_src(a))
-        send(f"xh{a}", t_at(0, 0, a), over_hi, t_src(a))
-        send(f"s0{a}", w_at(0, 0, a), sib, w_src(a))
-
-    acc[...] = jnp.zeros_like(acc)
-    for copy in small:
+    t_own("zua0", 0, up_z, t_a)
+    t_own("zdb0", 0, down_z, t_b)
+    w_own("yua", up_y, w_a)
+    w_own("ydb", down_y, w_b)
+    w_own("xa", over_lo, w_a)
+    t_own("xh0", 0, over_hi, t_all)
+    t_own("zub0", 0, up_z, t_b)
+    t_own("zda0", 0, down_z, t_a)
+    w_own("yub", up_y, w_b)
+    w_own("yda", down_y, w_a)
+    w_own("xb", over_lo, w_b)
+    t_own("xh1", 1, over_hi, t_all)
+    w_own("sa", sib, w_a)
+    w_own("sb", sib, w_b)
+    for copy in small + own:
         copy.wait()
     orbital = lax.broadcasted_iota(jnp.int32, pick.shape, 0)
     pick[...] = jnp.where(orbital == perm[...].reshape(1, V), 1.0, 0.0).T.astype(jnp.bfloat16)
 
-    def class_of(distance, other):
-        near = lax.rem(distance + 8, 4)
-        ring = jnp.where(near == 0, 1, jnp.where(near == 2, 3, 2))
-        return jnp.where(other == 0, 1, ring)
-
-    def multiply(stage):
-        def block(q, carry):
-            far = jnp.maximum(
-                class_of(q // 2 - y, lax.rem(q % 2 + xl, 2)),
-                class_of(q // 2 - z, lax.rem(q % 2 + xh, 2)),
+    acc[...] = jnp.zeros_like(acc)
+
+    def t_forward(j):
+        got(f"zua{j}")
+        send(f"zfu{j}", t_at(-1, 0, j, t_a), up_z)
+        got(f"zdb{j}")
+        send(f"zfd{j}", t_at(1, 0, j, t_b), down_z)
+
+    def t_partner(j):
+        got(f"xh{j}")
+        send(f"zpu{j}", t_at(0, 1, j, t_all), up_z)
+        send(f"zpd{j}", t_at(0, 1, j, t_all), down_z)
+
+    def t_forward_partner(j):
+        got(f"zpu{j}")
+        send(f"zgu{j}", t_at(-1, 1, j, t_a), up_z)
+        got(f"zpd{j}")
+        send(f"zgd{j}", t_at(1, 1, j, t_b), down_z)
+
+    def multiply(d, e, j):
+        q = slot(y + d, xl if e == 0 else 1 - xl)
+        cols = t_part(j, t_all)[1]
+
+        def tile(p, inner):
+            at = pl.ds(pl.multiple_of(p * TILE, TILE), TILE)
+            kept = mask[q, row * tiles + p].astype(jnp.float32)
+            acc[at, :] += kept * jnp.dot(
+                wb[q, at, :], tb[q, :, cols], preferred_element_type=jnp.float32
             )
-
-            @pl.when(far == stage)
-            def _():
-                def tile(p, inner):
-                    at = pl.ds(pl.multiple_of(p * TILE, TILE), TILE)
-                    kept = mask[q, row * tiles + p].astype(jnp.float32)
-                    acc[at, :] += kept * jnp.dot(
-                        wb[q, at, :], tb[q], preferred_element_type=jnp.float32
-                    )
-                    return inner
-
-                lax.fori_loop(0, tiles, tile, 0)
-
+            return inner
+
+        lax.fori_loop(0, tiles, tile, 0)
+
+    def multiply_ring(steps, e, j):
+        def one(n, carry):
+            multiply(steps[0] + n * steps[2], e, j)
             return carry
 
-        lax.fori_loop(0, 8, block, 0)
-
-    got("y+00")
-    send("fy+0", w_at(-1, 0, 0), up_y)
-    got("z+00")
-    send("fz+0", t_at(-1, 0, 0), up_z)
-    got("y-01")
-    send("fy-0", w_at(1, 0, 1), down_y)
-    got("z-01")
-    send("fz-0", t_at(1, 0, 1), down_z)
-    send("s-0", w_at(-1, 0, 0), sib)
-    send("s+1", w_at(1, 0, 1), sib)
-    for h in (0, 1):
-        got(f"xl{h}")
-        send(f"y+1{h}", w_at(0, 1, h), up_y)
-        send(f"y-1{h}", w_at(0, 1, h), down_y)
-        got(f"xh{h}")
-        send(f"z+1{h}", t_at(0, 1, h), up_z)
-        send(f"z-1{h}", t_at(0, 1, h), down_z)
-        send(f"sx{h}", w_at(0, 1, h), sib)
-        if h == 0:
-            got("y+01")
-            send("s-1", w_at(-1, 0, 1), sib)
-            got("y-00")
-            send("s+0", w_at(1, 0, 0), sib)
-            got("z+01")
-            got("z-00")
-    got("fy+0")
-    send("s20", w_at(2, 0, 0), sib)
-    got("fy-0")
-    send("s21", w_at(2, 0, 1), sib)
-    got("fz+0")
-    got("fz-0")
-    own_w.wait()
-    own_t.wait()
-    got("y+10")
-    send("fy+1", w_at(-1, 1, 0), up_y)
-    got("z+10")
-    send("fz+1", t_at(-1, 1, 0), up_z)
-    send("sx-0", w_at(-1, 1, 0), sib)
-    for name in ("s00", "s01", "s-0", "s-1", "s+0", "s+1", "sx0", "sx1", "s20", "s21"):
-        got(name)
-    multiply(1)
-    got("y-11")
-    send("fy-1", w_at(1, 1, 1), down_y)
-    got("z-11")
-    send("fz-1", t_at(1, 1, 1), down_z)
-    send("sx+1", w_at(1, 1, 1), sib)
-    got("y+11")
-    send("sx-1", w_at(-1, 1, 1), sib)
-    got("y-10")
-    send("sx+0", w_at(1, 1, 0), sib)
-    got("z+11")
-    got("z-10")
-    for name in ("sx-0", "sx-1", "sx+0", "sx+1"):
-        got(name)
-    multiply(2)
-    got("fy+1")
-    send("sx20", w_at(2, 1, 0), sib)
-    got("fy-1")
-    send("sx21", w_at(2, 1, 1), sib)
-    got("fz+1")
-    got("fz-1")
-    got("sx20")
-    got("sx21")
-    multiply(3)
+        lax.fori_loop(0, steps[1], one, 0)
 
     part = V // 4
     me = row * 16 + col
-    row_base = row * acc.shape[0]
-    col_base = col * acc.shape[1]
-
-    def block_at(t):
-        n = t // 2
-        hop = jnp.where(n == 0, 1, jnp.where(n == 1, 3, jnp.where(n == 2, 2, 0)))
-        return lax.rem(y + jnp.where(k == 0, hop, 4 - hop), 4), lax.rem(t + 1 + y, 2)
-
-    def exchange(t):
-        i, j = block_at(t)
+    row_base = row * comb.shape[0]
+    col_base = col * comb.shape[1]
+
+    def exchange(i, j):
         rows = pl.ds(pl.multiple_of(i * V, V), V)
         cols = pl.ds(pl.multiple_of(j * V, V), V)
         select = pick[...]
-        cyc = acc[rows, cols]
+        cyc = acc[rows, :]
         hi = cyc.astype(jnp.bfloat16)
         lo = (cyc - hi.astype(jnp.float32)).astype(jnp.bfloat16)
 
@@ -247,9 +202,8 @@
         comb[rows, cols] = combined
         comb_t[cols, rows] = combined.T
 
-    def pieces(t, s):
-        i, j = block_at(t)
-        n = t * 4 + s
+    def pieces(i, j, s):
+        n = (i * 2 + j) * 4 + s
         row_src = comb.at[
             pl.ds(pl.multiple_of(i * V + s * part, part), part), pl.ds(pl.multiple_of(j * V, V), V)
         ]
@@ -263,14 +217,15 @@
             (col_src, col_dst, col_sems.at[n], land_sems.at[1], col // 2, lax.rem(col, 2) * 8 + j * 4 + s),
         )
 
-    def each_piece(t, remote_step, local_step):
+    def each_piece(i, j, remote_step, local_step):
         def piece(s, carry):
-            for src, dst, sent, landed, to_row, to_col in pieces(t, s):
+            for src, dst, sent, landed, to_row, to_col in pieces(i, j, s):
                 here = to_row * 16 + to_col == me
-
-                @pl.when(here)
-                def _():
-                    local_step(pltpu.make_async_copy(src, dst, landed))
+                if local_step is not None:
+
+                    @pl.when(here)
+                    def _():
+                        local_step(pltpu.make_async_copy(src, dst, landed))
 
                 @pl.when(jnp.logical_not(here))
                 def _():
@@ -285,25 +240,93 @@
 
         lax.fori_loop(0, 4, piece, 0)
 
-    def start(t):
-        each_piece(t, lambda copy: copy.start(), lambda copy: copy.start())
-
-    def step(t, carry):
-        exchange(t)
-
-        @pl.when(t > 0)
-        def _():
-            start(t - 1)
-
-        return carry
-
-    lax.fori_loop(0, 8, step, 0)
-    start(7)
+    def start(i, j):
+        each_piece(i, j, lambda copy: copy.start(), lambda copy: copy.start())
+
+    def turned(u):
+        hop = jnp.where(u == 0, 1, jnp.where(u == 1, 3, jnp.where(u == 2, 2, 0)))
+        return lax.rem(y + jnp.where(k == 0, hop, 4 - hop), 4)
+
+    def leave(j):
+        def step(u, carry):
+            exchange(turned(u), j)
+
+            @pl.when(u > 0)
+            def _():
+                start(turned(u - 1), j)
+
+            return carry
+
+        lax.fori_loop(0, 4, step, 0)
+        start(turned(3), j)
+
+    t_forward(0)
+    got("yua")
+    send("fu", w_at(-1, 0, w_a), up_y)
+    send("sda", w_at(-1, 0, w_a), sib)
+    got("ydb")
+    send("fd", w_at(1, 0, w_b), down_y)
+    send("sub", w_at(1, 0, w_b), sib)
+    got("xa")
+    send("pua", w_at(0, 1, w_a), up_y)
+    send("pda", w_at(0, 1, w_a), down_y)
+    send("sxa", w_at(0, 1, w_a), sib)
+    t_partner(0)
+    t_own("zua1", 1, up_z, t_a)
+    t_own("zdb1", 1, down_z, t_b)
+    got("yub")
+    send("sdb", w_at(-1, 0, w_b), sib)
+    got("yda")
+    send("sua", w_at(1, 0, w_a), sib)
+    got("xb")
+    send("pub", w_at(0, 1, w_b), up_y)
+    send("pdb", w_at(0, 1, w_b), down_y)
+    send("sxb", w_at(0, 1, w_b), sib)
+    got("fu", "fd")
+    send("xf", w_at(2, 0, w_mid), over_lo)
+    send("sf", w_at(2, 0, (0, 2 * half)), sib)
+    t_forward_partner(0)
+    t_own("zub1", 1, up_z, t_b)
+    t_own("zda1", 1, down_z, t_a)
+    t_partner(1)
+    got("zub0", "zda0", "zfu0", "zfd0", "zgu0", "zgd0")
+    got("sa", "sb", "sda", "sdb", "sua", "sub", "sxa", "sxb", "sf")
+    multiply_ring((0, 2, 1), 0, 0)
+    got("pua")
+    send("gu", w_at(-1, 1, w_up), up_y)
+    send("sxda", w_at(-1, 1, w_a), sib)
+    t_forward(1)
+    multiply_ring((2, 2, 1), 0, 0)
+    got("pda")
+    send("sxua", w_at(1, 1, w_a), sib)
+    got("pdb")
+    send("gd", w_at(1, 1, w_down), down_y)
+    send("sxub", w_at(1, 1, w_b), sib)
+    got("pub")
+    send("sxdb", w_at(-1, 1, w_b), sib)
+    got("xf")
+    send("sxfm", w_at(2, 1, w_mid), sib)
+    multiply_ring((0, 1, 1), 1, 0)
+    t_forward_partner(1)
+    got("gu")
+    send("sxfu", w_at(2, 1, w_up), sib)
+    got("gd")
+    send("sxfd", w_at(2, 1, w_down), sib)
+    got("sxda", "sxdb", "sxua", "sxub")
+    multiply_ring((-1, 2, 2), 1, 0)
+    got("sxfm", "sxfu", "sxfd")
+    multiply_ring((2, 1, 1), 1, 0)
+    leave(first)
+    got("zub1", "zda1", "zfu1", "zfd1", "zgu1", "zgd1")
+    acc[...] = jnp.zeros_like(acc)
+    multiply_ring((0, 4, 1), 0, 1)
+    multiply_ring((0, 4, 1), 1, 1)
+    leave(second)
     for copy in copies.values():
         copy.wait_send()
 
     def sent(t, carry):
-        each_piece(t, lambda copy: copy.wait_send(), lambda copy: None)
+        each_piece(t // 2, lax.rem(t, 2), lambda copy: copy.wait_send(), None)
         return carry
 
     lax.fori_loop(0, 8, sent, 0)
@@ -377,14 +400,14 @@
         scratch_shapes=[
             pltpu.VMEM((8, row_count, 2 * depth), jnp.bfloat16),
             pltpu.VMEM((8, cycle_amps.shape[0], out_cols), jnp.bfloat16),
-            pltpu.VMEM((row_count, out_cols), jnp.float32),
+            pltpu.VMEM((row_count, V), jnp.float32),
             pltpu.VMEM((row_count, out_cols), jnp.bfloat16),
             pltpu.VMEM((out_cols, row_count), jnp.bfloat16),
             pltpu.VMEM((V, V), jnp.bfloat16),
             pltpu.SMEM(tile_mask.shape[::-1], jnp.int32),
             pltpu.VMEM((V,), jnp.int32),
-            pltpu.SemaphoreType.DMA((48,)),
-            pltpu.SemaphoreType.DMA((48,)),
+            pltpu.SemaphoreType.DMA((64,)),
+            pltpu.SemaphoreType.DMA((64,)),
             pltpu.SemaphoreType.DMA((4,)),
             pltpu.SemaphoreType.DMA((32,)),
             pltpu.SemaphoreType.DMA((32,)),

time: 157 us -> 163 us (1.038)
  the two profiles are of different devices: /device:TPU:3 before, /device:TPU:71 now
where the time goes in v4:
time: 163 us
  Pallas kernels  163 us (100%)
    pallas_call x1, Pallas kernels, on_device(): pl.pallas_call(cycle_kernel, name='cycle', out_shape=(jax.ShapeDtypeStruc...  160 us
    pallas_call x1, Pallas kernels, on_device(): pl.pallas_call(update_kernel, name='update', out_shape=jax.ShapeDtypeStru...  3.28 us

profile of v4, /device:TPU:71, one launch (start us, length us, event | category | flops | bytes accessed | tf_op | source)
XLA Modules:
  0.0 163.1 jit_solution(5312274308008375019)
XLA Ops:
  0.0 0.0 copy-start
  0.0 0.0 copy-start.1
  0.0 0.0 copy-start.2
  0.0 159.8 %cycle.1 = (bf16[96,12288]{1,0:T(8,128)(2,1)S(1)}, bf16[96,12288]{1,0:T(8,128)(2,1)S(1)}) custom-call(s32[8,16]{1,0:T(8,128)} %bitcast.1, s32[384]{0:T(512)} %perm_ref.1, bf16[1536,384]{1,0:T(8,128)(2,1)} %w_ref.1, bf16[768,768]{1,0:T(8,128)(2,1)} %t_ref.1), custom_call_target="tpu_custom_call" | custom-call | tf_op jit(solution)/shard_map/cycle/pallas_call | solution.py:394
  159.8 0.0 copy-done
  159.8 0.0 copy-done.1
  159.8 0.0 copy-done.2
  159.9 3.3 %update.1 = f32[96,12288]{1,0:T(8,128)} custom-call(bf16[96,12288]{1,0:T(8,128)(2,1)S(1)} %get-tuple-element.7.rows_ref, bf16[96,12288]{1,0:T(8,128)(2,1)S(1)} %get-tuple-element.8.cols_ref, bf16[96,12288]{1,0:T(8,128)(2,1)S(1)} %copy-done, f32[384]{0:T(512)S(1)} %copy-done.1, f32[32]{0:T(128)S(1)} %copy-done.2), custom_call_target="tpu_custom_call" | custom-call | tf_op jit(solution)/shard_map/update/pallas_call | solution.py:426
Async XLA Ops:
  0.0 159.8 %copy-start = (bf16[96,12288]{1,0:T(8,128)(2,1)S(1)}, bf16[96,12288]{1,0:T(8,128)(2,1)}, u32[]{:S(2)}) copy-start(bf16[96,12288]{1,0:T(8,128)(2,1)} %old_ref.1) | copy-start | bytes 7077892
  0.0 159.8 %copy-start.1 = (f32[384]{0:T(512)S(1)}, f32[384]{0:T(512)}, u32[]{:S(2)}) copy-start(f32[384]{0:T(512)} %virt_ref.1) | copy-start | bytes 4612
  0.0 159.8 %copy-start.2 = (f32[32]{0:T(128)S(1)}, f32[32]{0:T(128)}, u32[]{:S(2)}) copy-start(f32[32]{0:T(128)} %occ_ref.1) | copy-start | bytes 388

commit v5 on v3

--- a/solution.py
+++ b/solution.py
@@ -29,7 +29,6 @@
 ):
     row, col = lax.axis_index("row"), lax.axis_index("col")
     z, xh, y, xl, k = place()
-    half = {"w": wb.shape[1] // 2, "t": tb.shape[1] // 2}
     depth = w_ref.shape[1]
     tiles = acc.shape[0] // TILE
     k_cols = pl.ds(pl.multiple_of(k * depth, 128), depth)
@@ -68,13 +67,17 @@
     def slot(along, which):
         return lax.rem(along + 4, 4) * 2 + which
 
-    def w_at(dy, e, h):
-        e_xl = xl if e == 0 else 1 - xl
-        return wb.at[slot(y + dy, e_xl), pl.ds(h * half["w"], half["w"]), k_cols]
-
-    def t_at(dz, e, h):
-        e_xh = xh if e == 0 else 1 - xh
-        return tb.at[slot(z + dz, e_xh), pl.ds(h * half["t"], half["t"]), :]
+    half = wb.shape[1] // 2
+    w_parts = ((0, half), (half, half))
+    t_parts = ((0, V), (V, V))
+    w_far = ((0, 5 * half // 8), (5 * half // 8, 3 * half // 4), (11 * half // 8, 5 * half // 8))
+    t_far = ((0, 5 * V // 8), (5 * V // 8, 3 * V // 4), (11 * V // 8, 5 * V // 8))
+
+    def w_at(dy, e, part):
+        return wb.at[slot(y + dy, xl if e == 0 else 1 - xl), pl.ds(*part), k_cols]
+
+    def t_at(dz, e, part):
+        return tb.at[slot(z + dz, xh if e == 0 else 1 - xh), pl.ds(*part), :]
 
     copies = {}
 
@@ -90,8 +93,9 @@
         )
         copies[name].start()
 
-    def got(name):
-        copies[name].wait_recv()
+    def got(*names):
+        for name in names:
+            copies[name].wait_recv()
 
     own_w = pltpu.make_async_copy(w_ref, wb.at[slot(y, xl), :, k_cols], lsem.at[0])
     own_t = pltpu.make_async_copy(t_ref, tb.at[slot(z, xh)], lsem.at[1])
@@ -103,21 +107,16 @@
         copy.start()
     pl.semaphore_wait(barrier, expected)
 
-    def w_src(h):
-        return w_ref.at[pl.ds(h * half["w"], half["w"]), :]
-
-    def t_src(h):
-        return t_ref.at[pl.ds(h * half["t"], half["t"]), :]
-
     for first in (0, 1):
         a, b = first, 1 - first
-        send(f"y+0{a}", w_at(0, 0, a), up_y, w_src(a))
-        send(f"y-0{b}", w_at(0, 0, b), down_y, w_src(b))
-        send(f"z+0{a}", t_at(0, 0, a), up_z, t_src(a))
-        send(f"z-0{b}", t_at(0, 0, b), down_z, t_src(b))
-        send(f"xl{a}", w_at(0, 0, a), over_lo, w_src(a))
-        send(f"xh{a}", t_at(0, 0, a), over_hi, t_src(a))
-        send(f"s0{a}", w_at(0, 0, a), sib, w_src(a))
+        w_a, w_b, t_a, t_b = w_parts[a], w_parts[b], t_parts[a], t_parts[b]
+        send(f"y+0{a}", w_at(0, 0, w_a), up_y, w_ref.at[pl.ds(*w_a), :])
+        send(f"y-0{b}", w_at(0, 0, w_b), down_y, w_ref.at[pl.ds(*w_b), :])
+        send(f"z+0{a}", t_at(0, 0, t_a), up_z, t_ref.at[pl.ds(*t_a), :])
+        send(f"z-0{b}", t_at(0, 0, t_b), down_z, t_ref.at[pl.ds(*t_b), :])
+        send(f"xl{a}", w_at(0, 0, w_a), over_lo, w_ref.at[pl.ds(*w_a), :])
+        send(f"xh{a}", t_at(0, 0, t_a), over_hi, t_ref.at[pl.ds(*t_a), :])
+        send(f"s0{a}", w_at(0, 0, w_a), sib, w_ref.at[pl.ds(*w_a), :])
 
     acc[...] = jnp.zeros_like(acc)
     for copy in small:
@@ -130,93 +129,107 @@
         ring = jnp.where(near == 0, 1, jnp.where(near == 2, 3, 2))
         return jnp.where(other == 0, 1, ring)
 
-    def multiply(stage):
+    def farness(q):
+        return jnp.maximum(
+            class_of(q // 2 - y, lax.rem(q % 2 + xl, 2)),
+            class_of(q // 2 - z, lax.rem(q % 2 + xh, 2)),
+        )
+
+    def add_product(q, start, size):
+        at = pl.ds(pl.multiple_of(start, size), size)
+        kept = mask[q, row * tiles + start // TILE].astype(jnp.float32)
+        acc[at, :] += kept * jnp.dot(wb[q, at, :], tb[q], preferred_element_type=jnp.float32)
+
+    def multiply(stage, begin=0, end=8):
         def block(q, carry):
-            far = jnp.maximum(
-                class_of(q // 2 - y, lax.rem(q % 2 + xl, 2)),
-                class_of(q // 2 - z, lax.rem(q % 2 + xh, 2)),
-            )
-
-            @pl.when(far == stage)
+            @pl.when(farness(q) == stage)
             def _():
                 def tile(p, inner):
-                    at = pl.ds(pl.multiple_of(p * TILE, TILE), TILE)
-                    kept = mask[q, row * tiles + p].astype(jnp.float32)
-                    acc[at, :] += kept * jnp.dot(
-                        wb[q, at, :], tb[q], preferred_element_type=jnp.float32
-                    )
+                    add_product(q, p * TILE, TILE)
                     return inner
 
                 lax.fori_loop(0, tiles, tile, 0)
 
             return carry
 
+        lax.fori_loop(begin, end, block, 0)
+
+    def multiply_last(i):
+        def block(q, carry):
+            @pl.when(farness(q) == 3)
+            def _():
+                add_product(q, i * V, V)
+
+            return carry
+
         lax.fori_loop(0, 8, block, 0)
 
     got("y+00")
-    send("fy+0", w_at(-1, 0, 0), up_y)
+    send("fy+0", w_at(-1, 0, w_parts[0]), up_y)
     got("z+00")
-    send("fz+0", t_at(-1, 0, 0), up_z)
+    send("fz+0", t_at(-1, 0, t_parts[0]), up_z)
     got("y-01")
-    send("fy-0", w_at(1, 0, 1), down_y)
+    send("fy-0", w_at(1, 0, w_parts[1]), down_y)
     got("z-01")
-    send("fz-0", t_at(1, 0, 1), down_z)
-    send("s-0", w_at(-1, 0, 0), sib)
-    send("s+1", w_at(1, 0, 1), sib)
-    for h in (0, 1):
+    send("fz-0", t_at(1, 0, t_parts[1]), down_z)
+    send("s-0", w_at(-1, 0, w_parts[0]), sib)
+    send("s+1", w_at(1, 0, w_parts[1]), sib)
+
+    def w_partner(h):
         got(f"xl{h}")
-        send(f"y+1{h}", w_at(0, 1, h), up_y)
-        send(f"y-1{h}", w_at(0, 1, h), down_y)
+        send(f"y+1{h}", w_at(0, 1, w_parts[h]), up_y)
+        send(f"y-1{h}", w_at(0, 1, w_parts[h]), down_y)
+        send(f"sx{h}", w_at(0, 1, w_parts[h]), sib)
+
+    def t_partner(h):
         got(f"xh{h}")
-        send(f"z+1{h}", t_at(0, 1, h), up_z)
-        send(f"z-1{h}", t_at(0, 1, h), down_z)
-        send(f"sx{h}", w_at(0, 1, h), sib)
-        if h == 0:
-            got("y+01")
-            send("s-1", w_at(-1, 0, 1), sib)
-            got("y-00")
-            send("s+0", w_at(1, 0, 0), sib)
-            got("z+01")
-            got("z-00")
-    got("fy+0")
-    send("s20", w_at(2, 0, 0), sib)
-    got("fy-0")
-    send("s21", w_at(2, 0, 1), sib)
-    got("fz+0")
-    got("fz-0")
+        send(f"z+1{h}", t_at(0, 1, t_parts[h]), up_z)
+        send(f"z-1{h}", t_at(0, 1, t_parts[h]), down_z)
+
+    w_partner(0)
+    t_partner(0)
+    got("y+01")
+    send("s-1", w_at(-1, 0, w_parts[1]), sib)
+    got("y-00")
+    send("s+0", w_at(1, 0, w_parts[0]), sib)
+    got("z+01", "z-00")
+    w_partner(1)
+    got("fy+0", "fy-0")
+    send("xlf", w_at(2, 0, w_far[1]), over_lo)
+    send("s2", w_at(2, 0, (0, 2 * half)), sib)
+    got("fz+0", "fz-0")
+    send("xhf", t_at(2, 0, t_far[1]), over_hi)
+    t_partner(1)
+    got("y+10")
+    send("fy+1", w_at(-1, 1, w_far[0]), up_y)
+    got("z+10")
+    send("fz+1", t_at(-1, 1, t_far[0]), up_z)
+    send("sx-0", w_at(-1, 1, w_parts[0]), sib)
     own_w.wait()
     own_t.wait()
-    got("y+10")
-    send("fy+1", w_at(-1, 1, 0), up_y)
-    got("z+10")
-    send("fz+1", t_at(-1, 1, 0), up_z)
-    send("sx-0", w_at(-1, 1, 0), sib)
-    for name in ("s00", "s01", "s-0", "s-1", "s+0", "s+1", "sx0", "sx1", "s20", "s21"):
-        got(name)
+    got("s00", "s01", "s-0", "s-1", "s+0", "s+1", "sx0", "sx1", "s2")
     multiply(1)
     got("y-11")
-    send("fy-1", w_at(1, 1, 1), down_y)
+    send("fy-1", w_at(1, 1, w_far[2]), down_y)
     got("z-11")
-    send("fz-1", t_at(1, 1, 1), down_z)
-    send("sx+1", w_at(1, 1, 1), sib)
+    send("fz-1", t_at(1, 1, t_far[2]), down_z)
+    send("sx+1", w_at(1, 1, w_parts[1]), sib)
     got("y+11")
-    send("sx-1", w_at(-1, 1, 1), sib)
+    send("sx-1", w_at(-1, 1, w_parts[1]), sib)
     got("y-10")
-    send("sx+0", w_at(1, 1, 0), sib)
-    got("z+11")
-    got("z-10")
-    for name in ("sx-0", "sx-1", "sx+0", "sx+1"):
-        got(name)
-    multiply(2)
+    send("sx+0", w_at(1, 1, w_parts[0]), sib)
+    got("z+11", "z-10")
+    got("sx-0", "sx-1", "sx+0", "sx+1")
+    multiply(2, 0, 4)
     got("fy+1")
-    send("sx20", w_at(2, 1, 0), sib)
+    send("sf0", w_at(2, 1, w_far[0]), sib)
+    got("xlf")
+    send("sf1", w_at(2, 1, w_far[1]), sib)
     got("fy-1")
-    send("sx21", w_at(2, 1, 1), sib)
-    got("fz+1")
-    got("fz-1")
-    got("sx20")
-    got("sx21")
-    multiply(3)
+    send("sf2", w_at(2, 1, w_far[2]), sib)
+    multiply(2, 4, 8)
+    got("fz+1", "fz-1", "xhf")
+    got("sf0", "sf1", "sf2")
 
     part = V // 4
     me = row * 16 + col
@@ -230,6 +243,11 @@
 
     def exchange(t):
         i, j = block_at(t)
+
+        @pl.when(lax.rem(t, 2) == 0)
+        def _():
+            multiply_last(i)
+
         rows = pl.ds(pl.multiple_of(i * V, V), V)
         cols = pl.ds(pl.multiple_of(j * V, V), V)
         select = pick[...]

time: 157 us -> 151 us (0.962); the launches traced: 156 us -> 149 us
  Pallas kernels: 156 us -> 149 us
    pallas_call x1, Pallas kernels: 153 us -> 145 us  [on_device(): pl.pallas_call(cycle_kernel, name='cycle', out_shape=(jax.ShapeDtypeStruc...]
where the time goes in v5:
time: 151 us; the launch traced here: 149 us
  Pallas kernels  149 us (99%)
    pallas_call x1, Pallas kernels, on_device(): pl.pallas_call(cycle_kernel, name='cycle', out_shape=(jax.ShapeDtypeStruc...  145 us
    pallas_call x1, Pallas kernels, on_device(): pl.pallas_call(update_kernel, name='update', out_shape=jax.ShapeDtypeStru...  3.28 us

profile of v5, /device:TPU:3, one launch (start us, length us, event | category | flops | bytes accessed | tf_op | source)
XLA Modules:
  0.0 148.7 jit_solution(16592478300601996935)
XLA Ops:
  0.0 0.0 copy-start
  0.0 0.0 copy-start.1
  0.0 0.0 copy-start.2
  0.0 145.4 %cycle.1 = (bf16[96,12288]{1,0:T(8,128)(2,1)S(1)}, bf16[96,12288]{1,0:T(8,128)(2,1)S(1)}) custom-call(s32[8,16]{1,0:T(8,128)} %bitcast.1, s32[384]{0:T(512)} %perm_ref.1, bf16[1536,384]{1,0:T(8,128)(2,1)} %w_ref.1, bf16[768,768]{1,0:T(8,128)(2,1)} %t_ref.1), custom_call_target="tpu_custom_call" | custom-call | tf_op jit(solution)/shard_map/cycle/pallas_call | solution.py:389
  145.4 0.0 copy-done
  145.4 0.0 copy-done.1
  145.4 0.0 copy-done.2
  145.4 3.3 %update.1 = f32[96,12288]{1,0:T(8,128)} custom-call(bf16[96,12288]{1,0:T(8,128)(2,1)S(1)} %get-tuple-element.7.rows_ref, bf16[96,12288]{1,0:T(8,128)(2,1)S(1)} %get-tuple-element.8.cols_ref, bf16[96,12288]{1,0:T(8,128)(2,1)S(1)} %copy-done, f32[384]{0:T(512)S(1)} %copy-done.1, f32[32]{0:T(128)S(1)} %copy-done.2), custom_call_target="tpu_custom_call" | custom-call | tf_op jit(solution)/shard_map/update/pallas_call | solution.py:421
Async XLA Ops:
  0.0 145.4 %copy-start = (bf16[96,12288]{1,0:T(8,128)(2,1)S(1)}, bf16[96,12288]{1,0:T(8,128)(2,1)}, u32[]{:S(2)}) copy-start(bf16[96,12288]{1,0:T(8,128)(2,1)} %old_ref.1) | copy-start | bytes 7077892
  0.0 145.4 %copy-start.1 = (f32[384]{0:T(512)S(1)}, f32[384]{0:T(512)}, u32[]{:S(2)}) copy-start(f32[384]{0:T(512)} %virt_ref.1) | copy-start | bytes 4612
  0.0 145.4 %copy-start.2 = (f32[32]{0:T(128)S(1)}, f32[32]{0:T(128)}, u32[]{:S(2)}) copy-start(f32[32]{0:T(128)} %occ_ref.1) | copy-start | bytes 388

commit v6 on v5

--- a/solution.py
+++ b/solution.py
@@ -25,7 +25,7 @@
 def cycle_kernel(
     mask_ref, perm_ref, w_ref, t_ref,
     rows_ref, cols_ref,
-    wb, tb, acc, comb, comb_t, pick, mask, perm, ssem, rsem, lsem, row_sems, col_sems, land_sems,
+    wb, tb, acc, comb, comb_t, pick, mask, perm, ssem, rsem, lsem, row_sems, col_sems, land_sems, near_sems,
 ):
     row, col = lax.axis_index("row"), lax.axis_index("col")
     z, xh, y, xl, k = place()
@@ -41,28 +41,9 @@
 
     barrier = pltpu.get_barrier_semaphore()
 
-    def greet(peer):
+    peers = (up_y, down_y, up_z, down_z, over_lo, over_hi, sib)
+    for peer in peers:
         pl.semaphore_signal(barrier, inc=1, device_id=peer, device_id_type=MESH)
-
-    for peer in (up_z, down_z, over_hi):
-        greet(peer)
-
-    def greet_row(step, carry):
-        greet((row, lax.rem(col + step, 16)))
-        return carry
-
-    lax.fori_loop(1, 16, greet_row, 0)
-    col_source = 2 * row + col // 8
-
-    def greet_source(step, carry):
-        @pl.when(jnp.logical_or(step != row, col_source != col))
-        def _():
-            greet((step, col_source))
-
-        return carry
-
-    lax.fori_loop(0, 8, greet_source, 0)
-    expected = 3 + 15 + 8 - jnp.where(col_source == col, 1, 0)
 
     def slot(along, which):
         return lax.rem(along + 4, 4) * 2 + which
@@ -105,7 +86,7 @@
     )
     for copy in (*small, own_w, own_t):
         copy.start()
-    pl.semaphore_wait(barrier, expected)
+    pl.semaphore_wait(barrier, len(peers))
 
     for first in (0, 1):
         a, b = first, 1 - first
@@ -156,13 +137,23 @@
 
     def multiply_last(i):
         def block(q, carry):
-            @pl.when(farness(q) == 3)
+            far = farness(q)
+
+            @pl.when(jnp.logical_or(far == 3, jnp.logical_and(far == 2, q >= 4)))
             def _():
                 add_product(q, i * V, V)
 
             return carry
 
         lax.fori_loop(0, 8, block, 0)
+
+    def spread(n, carry):
+        for peer in peers:
+            pl.semaphore_signal(near_sems.at[n], inc=1, device_id=peer, device_id_type=MESH)
+        pl.semaphore_wait(near_sems.at[n], len(peers))
+        return carry
+
+    lax.fori_loop(0, 6, spread, 0)
 
     got("y+00")
     send("fy+0", w_at(-1, 0, w_parts[0]), up_y)
@@ -227,7 +218,6 @@
     send("sf1", w_at(2, 1, w_far[1]), sib)
     got("fy-1")
     send("sf2", w_at(2, 1, w_far[2]), sib)
-    multiply(2, 4, 8)
     got("fz+1", "fz-1", "xhf")
     got("sf0", "sf1", "sf2")
 
@@ -308,15 +298,10 @@
 
     def step(t, carry):
         exchange(t)
-
-        @pl.when(t > 0)
-        def _():
-            start(t - 1)
-
+        start(t)
         return carry
 
     lax.fori_loop(0, 8, step, 0)
-    start(7)
     for copy in copies.values():
         copy.wait_send()
 
@@ -407,6 +392,7 @@
             pltpu.SemaphoreType.DMA((32,)),
             pltpu.SemaphoreType.DMA((32,)),
             pltpu.SemaphoreType.DMA((2,)),
+            pltpu.SemaphoreType.REGULAR((6,)),
         ],
         compiler_params=pltpu.CompilerParams(
             collective_id=1, has_side_effects=True, vmem_limit_bytes=44 * 1024 * 1024

time: 151 us -> 147 us (0.974); the launches traced: 149 us -> 146 us
  Pallas kernels: 149 us -> 146 us
    pallas_call x1, Pallas kernels: 145 us -> 143 us  [on_device(): pl.pallas_call(cycle_kernel, name='cycle', out_shape=(jax.ShapeDtypeStruc...]
where the time goes in v6:
time: 147 us; the launch traced here: 146 us
  Pallas kernels  146 us (99%)
    pallas_call x1, Pallas kernels, on_device(): pl.pallas_call(cycle_kernel, name='cycle', out_shape=(jax.ShapeDtypeStruc...  143 us
    pallas_call x1, Pallas kernels, on_device(): pl.pallas_call(update_kernel, name='update', out_shape=jax.ShapeDtypeStru...  3.28 us

profile of v6, /device:TPU:3, one launch (start us, length us, event | category | flops | bytes accessed | tf_op | source)
XLA Modules:
  0.0 146.3 jit_solution(9136136592447570348)
XLA Ops:
  0.0 0.0 copy-start
  0.0 0.0 copy-start.1
  0.0 0.0 copy-start.2
  0.0 143.0 %cycle.1 = (bf16[96,12288]{1,0:T(8,128)(2,1)S(1)}, bf16[96,12288]{1,0:T(8,128)(2,1)S(1)}) custom-call(s32[8,16]{1,0:T(8,128)} %bitcast.1, s32[384]{0:T(512)} %perm_ref.1, bf16[1536,384]{1,0:T(8,128)(2,1)} %w_ref.1, bf16[768,768]{1,0:T(8,128)(2,1)} %t_ref.1), custom_call_target="tpu_custom_call" | custom-call | tf_op jit(solution)/shard_map/cycle/pallas_call | solution.py:374
  143.0 0.0 copy-done
  143.0 0.0 copy-done.1
  143.0 0.0 copy-done.2
  143.1 3.3 %update.1 = f32[96,12288]{1,0:T(8,128)} custom-call(bf16[96,12288]{1,0:T(8,128)(2,1)S(1)} %get-tuple-element.7.rows_ref, bf16[96,12288]{1,0:T(8,128)(2,1)S(1)} %get-tuple-element.8.cols_ref, bf16[96,12288]{1,0:T(8,128)(2,1)S(1)} %copy-done, f32[384]{0:T(512)S(1)} %copy-done.1, f32[32]{0:T(128)S(1)} %copy-done.2), custom_call_target="tpu_custom_call" | custom-call | tf_op jit(solution)/shard_map/update/pallas_call | solution.py:407
Async XLA Ops:
  0.0 143.0 %copy-start = (bf16[96,12288]{1,0:T(8,128)(2,1)S(1)}, bf16[96,12288]{1,0:T(8,128)(2,1)}, u32[]{:S(2)}) copy-start(bf16[96,12288]{1,0:T(8,128)(2,1)} %old_ref.1) | copy-start | bytes 7077892
  0.0 143.0 %copy-start.1 = (f32[384]{0:T(512)S(1)}, f32[384]{0:T(512)}, u32[]{:S(2)}) copy-start(f32[384]{0:T(512)} %virt_ref.1) | copy-start | bytes 4612
  0.0 143.0 %copy-start.2 = (f32[32]{0:T(128)S(1)}, f32[32]{0:T(128)}, u32[]{:S(2)}) copy-start(f32[32]{0:T(128)} %occ_ref.1) | copy-start | bytes 388

commit v7 on v6

--- a/solution.py
+++ b/solution.py
@@ -51,8 +51,10 @@
     half = wb.shape[1] // 2
     w_parts = ((0, half), (half, half))
     t_parts = ((0, V), (V, V))
-    w_far = ((0, 5 * half // 8), (5 * half // 8, 3 * half // 4), (11 * half // 8, 5 * half // 8))
-    t_far = ((0, 5 * V // 8), (5 * V // 8, 3 * V // 4), (11 * V // 8, 5 * V // 8))
+    w_far = ((0, 288), (576, 960), (288, 288))
+    t_far = ((0, 288), (576, 192), (288, 288))
+    w_cross = {"0": (0, half), "1": (half, half // 2), "2": (3 * half // 2, half // 2)}
+    t_cross = {"0": (0, V), "1": (V, V // 2), "2": (3 * V // 2, V // 2)}
 
     def w_at(dy, e, part):
         return wb.at[slot(y + dy, xl if e == 0 else 1 - xl), pl.ds(*part), k_cols]
@@ -95,8 +97,10 @@
         send(f"y-0{b}", w_at(0, 0, w_b), down_y, w_ref.at[pl.ds(*w_b), :])
         send(f"z+0{a}", t_at(0, 0, t_a), up_z, t_ref.at[pl.ds(*t_a), :])
         send(f"z-0{b}", t_at(0, 0, t_b), down_z, t_ref.at[pl.ds(*t_b), :])
-        send(f"xl{a}", w_at(0, 0, w_a), over_lo, w_ref.at[pl.ds(*w_a), :])
-        send(f"xh{a}", t_at(0, 0, t_a), over_hi, t_ref.at[pl.ds(*t_a), :])
+        for h in ("0",) if first == 0 else ("1", "2"):
+            w_h, t_h = w_cross[h], t_cross[h]
+            send(f"xl{h}", w_at(0, 0, w_h), over_lo, w_ref.at[pl.ds(*w_h), :])
+            send(f"xh{h}", t_at(0, 0, t_h), over_hi, t_ref.at[pl.ds(*t_h), :])
         send(f"s0{a}", w_at(0, 0, w_a), sib, w_ref.at[pl.ds(*w_a), :])
 
     acc[...] = jnp.zeros_like(acc)
@@ -108,7 +112,7 @@
     def class_of(distance, other):
         near = lax.rem(distance + 8, 4)
         ring = jnp.where(near == 0, 1, jnp.where(near == 2, 3, 2))
-        return jnp.where(other == 0, 1, ring)
+        return jnp.where(other == 0, 0, ring)
 
     def farness(q):
         return jnp.maximum(
@@ -135,11 +139,19 @@
 
         lax.fori_loop(begin, end, block, 0)
 
-    def multiply_last(i):
+    def block_at(t):
+        n = t // 2
+        hop = jnp.where(n == 0, 1, jnp.where(n == 1, 3, jnp.where(n == 2, 2, 0)))
+        return lax.rem(y + jnp.where(k == 0, hop, 4 - hop), 4), lax.rem(t + 1 + y, 2)
+
+    late = slot(z + 2, 1 - xh)
+
+    def multiply_rest(i):
         def block(q, carry):
             far = farness(q)
-
-            @pl.when(jnp.logical_or(far == 3, jnp.logical_and(far == 2, q >= 4)))
+            left = jnp.logical_or(far == 3, jnp.logical_and(far == 2, q >= 4))
+
+            @pl.when(jnp.logical_and(left, q != late))
             def _():
                 add_product(q, i * V, V)
 
@@ -168,49 +180,59 @@
 
     def w_partner(h):
         got(f"xl{h}")
-        send(f"y+1{h}", w_at(0, 1, w_parts[h]), up_y)
-        send(f"y-1{h}", w_at(0, 1, w_parts[h]), down_y)
-        send(f"sx{h}", w_at(0, 1, w_parts[h]), sib)
+        send(f"y+1{h}", w_at(0, 1, w_cross[h]), up_y)
+        send(f"y-1{h}", w_at(0, 1, w_cross[h]), down_y)
+        send(f"sx{h}", w_at(0, 1, w_cross[h]), sib)
 
     def t_partner(h):
         got(f"xh{h}")
-        send(f"z+1{h}", t_at(0, 1, t_parts[h]), up_z)
-        send(f"z-1{h}", t_at(0, 1, t_parts[h]), down_z)
-
-    w_partner(0)
-    t_partner(0)
+        send(f"z+1{h}", t_at(0, 1, t_cross[h]), up_z)
+        send(f"z-1{h}", t_at(0, 1, t_cross[h]), down_z)
+
+    w_partner("0")
+    t_partner("0")
     got("y+01")
     send("s-1", w_at(-1, 0, w_parts[1]), sib)
     got("y-00")
     send("s+0", w_at(1, 0, w_parts[0]), sib)
     got("z+01", "z-00")
-    w_partner(1)
-    got("fy+0", "fy-0")
+    w_partner("1")
+    t_partner("1")
+    got("fy-0", "fy+0")
     send("xlf", w_at(2, 0, w_far[1]), over_lo)
+    got("fz-0")
+    send("xhf", t_at(2, 0, t_far[1]), over_hi)
+    got("fz+0")
     send("s2", w_at(2, 0, (0, 2 * half)), sib)
-    got("fz+0", "fz-0")
-    send("xhf", t_at(2, 0, t_far[1]), over_hi)
-    t_partner(1)
+    own_w.wait()
+    own_t.wait()
+    got("s00", "s01", "s-0", "s-1", "s+0", "s+1", "s2")
+    multiply(0)
+    w_partner("2")
+    t_partner("2")
     got("y+10")
     send("fy+1", w_at(-1, 1, w_far[0]), up_y)
     got("z+10")
     send("fz+1", t_at(-1, 1, t_far[0]), up_z)
-    send("sx-0", w_at(-1, 1, w_parts[0]), sib)
-    own_w.wait()
-    own_t.wait()
-    got("s00", "s01", "s-0", "s-1", "s+0", "s+1", "sx0", "sx1", "s2")
-    multiply(1)
+    send("sx-0", w_at(-1, 1, w_cross["0"]), sib)
+    got("y-10")
+    send("sx+0", w_at(1, 1, w_cross["0"]), sib)
+    got("z-10")
     got("y-11")
     send("fy-1", w_at(1, 1, w_far[2]), down_y)
     got("z-11")
     send("fz-1", t_at(1, 1, t_far[2]), down_z)
-    send("sx+1", w_at(1, 1, w_parts[1]), sib)
+    send("sx+1", w_at(1, 1, w_cross["1"]), sib)
+    got("sx0", "sx1", "sx2")
+    multiply(1)
     got("y+11")
-    send("sx-1", w_at(-1, 1, w_parts[1]), sib)
-    got("y-10")
-    send("sx+0", w_at(1, 1, w_parts[0]), sib)
-    got("z+11", "z-10")
-    got("sx-0", "sx-1", "sx+0", "sx+1")
+    send("sx-1", w_at(-1, 1, w_cross["1"]), sib)
+    got("y+12")
+    send("sx-2", w_at(-1, 1, w_cross["2"]), sib)
+    got("y-12")
+    send("sx+2", w_at(1, 1, w_cross["2"]), sib)
+    got("z+11", "z+12", "z-12")
+    got("sx-0", "sx-1", "sx-2", "sx+0", "sx+1", "sx+2")
     multiply(2, 0, 4)
     got("fy+1")
     send("sf0", w_at(2, 1, w_far[0]), sib)
@@ -218,25 +240,25 @@
     send("sf1", w_at(2, 1, w_far[1]), sib)
     got("fy-1")
     send("sf2", w_at(2, 1, w_far[2]), sib)
+    got("sf0", "sf1", "sf2")
+    multiply_rest(block_at(0)[0])
     got("fz+1", "fz-1", "xhf")
-    got("sf0", "sf1", "sf2")
 
     part = V // 4
     me = row * 16 + col
     row_base = row * acc.shape[0]
     col_base = col * acc.shape[1]
 
-    def block_at(t):
-        n = t // 2
-        hop = jnp.where(n == 0, 1, jnp.where(n == 1, 3, jnp.where(n == 2, 2, 0)))
-        return lax.rem(y + jnp.where(k == 0, hop, 4 - hop), 4), lax.rem(t + 1 + y, 2)
-
     def exchange(t):
         i, j = block_at(t)
 
+        @pl.when(jnp.logical_and(lax.rem(t, 2) == 0, t >= 2))
+        def _():
+            multiply_rest(i)
+
         @pl.when(lax.rem(t, 2) == 0)
         def _():
-            multiply_last(i)
+            add_product(late, i * V, V)
 
         rows = pl.ds(pl.multiple_of(i * V, V), V)
         cols = pl.ds(pl.multiple_of(j * V, V), V)
@@ -386,8 +408,8 @@
             pltpu.VMEM((V, V), jnp.bfloat16),
             pltpu.SMEM(tile_mask.shape[::-1], jnp.int32),
             pltpu.VMEM((V,), jnp.int32),
-            pltpu.SemaphoreType.DMA((48,)),
-            pltpu.SemaphoreType.DMA((48,)),
+            pltpu.SemaphoreType.DMA((64,)),
+            pltpu.SemaphoreType.DMA((64,)),
             pltpu.SemaphoreType.DMA((4,)),
             pltpu.SemaphoreType.DMA((32,)),
             pltpu.SemaphoreType.DMA((32,)),

time: 147 us -> 146 us (level)
  no operation moved by 1% of the time
where the time goes in v7:
time: 146 us
  Pallas kernels  146 us (100%)
    pallas_call x1, Pallas kernels, on_device(): pl.pallas_call(cycle_kernel, name='cycle', out_shape=(jax.ShapeDtypeStruc...  142 us
    pallas_call x1, Pallas kernels, on_device(): pl.pallas_call(update_kernel, name='update', out_shape=jax.ShapeDtypeStru...  3.28 us

profile of v7, /device:TPU:3, one launch (start us, length us, event | category | flops | bytes accessed | tf_op | source)
XLA Modules:
  0.0 145.7 jit_solution(5891155516447925936)
XLA Ops:
  0.0 0.0 copy-start
  0.0 0.0 copy-start.1
  0.0 0.0 copy-start.2
  0.0 142.4 %cycle.1 = (bf16[96,12288]{1,0:T(8,128)(2,1)S(1)}, bf16[96,12288]{1,0:T(8,128)(2,1)S(1)}) custom-call(s32[8,16]{1,0:T(8,128)} %bitcast.1, s32[384]{0:T(512)} %perm_ref.1, bf16[1536,384]{1,0:T(8,128)(2,1)} %w_ref.1, bf16[768,768]{1,0:T(8,128)(2,1)} %t_ref.1), custom_call_target="tpu_custom_call" | custom-call | tf_op jit(solution)/shard_map/cycle/pallas_call | solution.py:396
  142.4 0.0 copy-done
  142.4 0.0 copy-done.1
  142.4 0.0 copy-done.2
  142.4 3.3 %update.1 = f32[96,12288]{1,0:T(8,128)} custom-call(bf16[96,12288]{1,0:T(8,128)(2,1)S(1)} %get-tuple-element.7.rows_ref, bf16[96,12288]{1,0:T(8,128)(2,1)S(1)} %get-tuple-element.8.cols_ref, bf16[96,12288]{1,0:T(8,128)(2,1)S(1)} %copy-done, f32[384]{0:T(512)S(1)} %copy-done.1, f32[32]{0:T(128)S(1)} %copy-done.2), custom_call_target="tpu_custom_call" | custom-call | tf_op jit(solution)/shard_map/update/pallas_call | solution.py:429
Async XLA Ops:
  0.0 142.4 %copy-start = (bf16[96,12288]{1,0:T(8,128)(2,1)S(1)}, bf16[96,12288]{1,0:T(8,128)(2,1)}, u32[]{:S(2)}) copy-start(bf16[96,12288]{1,0:T(8,128)(2,1)} %old_ref.1) | copy-start | bytes 7077892
  0.0 142.4 %copy-start.1 = (f32[384]{0:T(512)S(1)}, f32[384]{0:T(512)}, u32[]{:S(2)}) copy-start(f32[384]{0:T(512)} %virt_ref.1) | copy-start | bytes 4612
  0.0 142.4 %copy-start.2 = (f32[32]{0:T(128)S(1)}, f32[32]{0:T(128)}, u32[]{:S(2)}) copy-start(f32[32]{0:T(128)} %occ_ref.1) | copy-start | bytes 388

commit v8 on v7

--- a/solution.py
+++ b/solution.py
@@ -51,7 +51,7 @@
     half = wb.shape[1] // 2
     w_parts = ((0, half), (half, half))
     t_parts = ((0, V), (V, V))
-    w_far = ((0, 288), (576, 960), (288, 288))
+    w_far = ((0, 336), (672, 864), (336, 336))
     t_far = ((0, 288), (576, 192), (288, 288))
     w_cross = {"0": (0, half), "1": (half, half // 2), "2": (3 * half // 2, half // 2)}
     t_cross = {"0": (0, V), "1": (V, V // 2), "2": (3 * V // 2, V // 2)}
@@ -140,9 +140,9 @@
         lax.fori_loop(begin, end, block, 0)
 
     def block_at(t):
-        n = t // 2
+        n = t // 4 * 2 + lax.rem(t, 2)
         hop = jnp.where(n == 0, 1, jnp.where(n == 1, 3, jnp.where(n == 2, 2, 0)))
-        return lax.rem(y + jnp.where(k == 0, hop, 4 - hop), 4), lax.rem(t + 1 + y, 2)
+        return lax.rem(y + jnp.where(k == 0, hop, 4 - hop), 4), lax.rem(t // 2 + t + 1 + y, 2)
 
     late = slot(z + 2, 1 - xh)
 
@@ -252,11 +252,13 @@
     def exchange(t):
         i, j = block_at(t)
 
-        @pl.when(jnp.logical_and(lax.rem(t, 2) == 0, t >= 2))
+        fresh = lax.rem(t // 2, 2) == 0
+
+        @pl.when(jnp.logical_and(fresh, t > 0))
         def _():
             multiply_rest(i)
 
-        @pl.when(lax.rem(t, 2) == 0)
+        @pl.when(fresh)
         def _():
             add_product(late, i * V, V)
 
@@ -336,51 +338,35 @@
     pltpu.make_async_copy(cols_ref, cols_ref, land_sems.at[1]).wait()
 
 
-def update_kernel(
-    rows_ref, cols_ref, old_ref, virt_ref, occ_ref, out_ref, old, out, virt, occ, in_sems, out_sems
-):
-    slab_rows = old.shape[0]
-    chunks = in_sems.shape[0] - 2
-    width = old.shape[1] // chunks
+def update_kernel(rows_ref, cols_ref, old_ref, virt_ref, occ_ref, out_ref, out, occ, in_sem, out_sems):
+    slab_rows, total_cols = old_ref.shape
+    chunks = out_sems.shape[0]
+    width = total_cols // chunks
     slab = lax.axis_index("row") * 16 + lax.axis_index("col")
-    small = (
-        pltpu.make_async_copy(virt_ref, virt, in_sems.at[chunks]),
-        pltpu.make_async_copy(occ_ref, occ, in_sems.at[chunks + 1]),
-    )
-    for copy in small:
-        copy.start()
+    energies = pltpu.make_async_copy(occ_ref, occ, in_sem.at[0])
+    energies.start()
 
     def chunk_of(n):
         return (slice(None), pl.ds(n * width, width))
 
-    reads = [
-        pltpu.make_async_copy(old_ref.at[chunk_of(n)], old.at[chunk_of(n)], in_sems.at[n])
-        for n in range(chunks)
-    ]
     writes = [
         pltpu.make_async_copy(out.at[chunk_of(n)], out_ref.at[chunk_of(n)], out_sems.at[n])
         for n in range(chunks)
     ]
-    for copy in reads:
-        copy.start()
-    for copy in small:
-        copy.wait()
     per_orbital = V // slab_rows
-    virtual = virt[...].reshape(1, V)
+    virtual = virt_ref[...].reshape(1, V)
     lanes = lax.broadcasted_iota(jnp.int32, (slab_rows, V), 1)
     wanted = lax.broadcasted_iota(jnp.int32, (slab_rows, V), 0) + lax.rem(slab, per_orbital) * slab_rows
-    row_energy = (
-        jnp.sum(jnp.where(lanes == wanted, virtual, 0.0), axis=1, keepdims=True)
-        - occ[slab // per_orbital]
-    )
+    row_energy = jnp.sum(jnp.where(lanes == wanted, virtual, 0.0), axis=1, keepdims=True)
+    energies.wait()
+    row_energy = row_energy - occ[slab // per_orbital]
     for n in range(chunks):
-        reads[n].wait()
 
         def orbital(j, carry):
             cols = pl.ds(pl.multiple_of(j * V, V), V)
             denominator = row_energy + (virtual - occ[j])
             paired = rows_ref[:, cols].astype(jnp.float32) + cols_ref[:, cols].astype(jnp.float32)
-            out[:, cols] = old[:, cols].astype(jnp.float32) + paired / denominator
+            out[:, cols] = old_ref[:, cols].astype(jnp.float32) + paired / denominator
             return carry
 
         lax.fori_loop(n * (width // V), (n + 1) * (width // V), orbital, 0)
@@ -425,19 +411,17 @@
             for operand in (tile_mask.T, virt_perm, interaction, cycle_amps)
         )
     )
-    chunks = 4
+    chunks = 8
     return pl.pallas_call(
         update_kernel,
         name="update",
         out_shape=jax.ShapeDtypeStruct((slab_rows, total_cols), jnp.float32),
-        in_specs=[pl.BlockSpec(memory_space=pltpu.VMEM)] * 2 + [pl.BlockSpec(memory_space=pltpu.HBM)] * 3,
+        in_specs=[pl.BlockSpec(memory_space=pltpu.VMEM)] * 4 + [pl.BlockSpec(memory_space=pltpu.HBM)],
         out_specs=pl.BlockSpec(memory_space=pltpu.HBM),
         scratch_shapes=[
-            pltpu.VMEM((slab_rows, total_cols), jnp.bfloat16),
             pltpu.VMEM((slab_rows, total_cols), jnp.float32),
-            pltpu.VMEM((V,), jnp.float32),
             pltpu.SMEM((occ_energy.shape[0],), jnp.float32),
-            pltpu.SemaphoreType.DMA((chunks + 2,)),
+            pltpu.SemaphoreType.DMA((1,)),
             pltpu.SemaphoreType.DMA((chunks,)),
         ],
         compiler_params=pltpu.CompilerParams(vmem_limit_bytes=12 * 1024 * 1024),

time: 146 us -> 145 us (level); the launches traced: 146 us -> 142 us
  Pallas kernels: 146 us -> 142 us
    pallas_call x1, Pallas kernels: 142 us -> 139 us  [on_device(): pl.pallas_call(cycle_kernel, name='cycle', out_shape=(jax.ShapeDtypeStruc...]
where the time goes in v8:
time: 145 us; the launch traced here: 142 us
  Pallas kernels  142 us (98%)
    pallas_call x1, Pallas kernels, on_device(): pl.pallas_call(cycle_kernel, name='cycle', out_shape=(jax.ShapeDtypeStruc...  139 us
    pallas_call x1, Pallas kernels, on_device(): pl.pallas_call(update_kernel, name='update', out_shape=jax.ShapeDtypeStru...  3 us

profile of v8, /device:TPU:3, one launch (start us, length us, event | category | flops | bytes accessed | tf_op | source)
XLA Modules:
  0.0 141.8 jit_solution(3187836660245322605)
XLA Ops:
  0.0 0.0 copy-start
  0.0 0.0 copy-start.1
  0.0 0.0 copy-start.2
  0.0 138.7 %cycle.1 = (bf16[96,12288]{1,0:T(8,128)(2,1)S(1)}, bf16[96,12288]{1,0:T(8,128)(2,1)S(1)}) custom-call(s32[8,16]{1,0:T(8,128)} %bitcast.1, s32[384]{0:T(512)} %perm_ref.1, bf16[1536,384]{1,0:T(8,128)(2,1)} %w_ref.1, bf16[768,768]{1,0:T(8,128)(2,1)} %t_ref.1), custom_call_target="tpu_custom_call" | custom-call | tf_op jit(solution)/shard_map/cycle/pallas_call | solution.py:382
  138.8 0.0 copy-done
  138.8 0.0 copy-done.1
  138.8 0.0 copy-done.2
  138.8 3.0 %update.1 = f32[96,12288]{1,0:T(8,128)} custom-call(bf16[96,12288]{1,0:T(8,128)(2,1)S(1)} %get-tuple-element.7.rows_ref, bf16[96,12288]{1,0:T(8,128)(2,1)S(1)} %get-tuple-element.8.cols_ref, bf16[96,12288]{1,0:T(8,128)(2,1)S(1)} %copy-done, f32[384]{0:T(512)S(1)} %copy-done.1, f32[32]{0:T(128)S(1)} %copy-done.2), custom_call_target="tpu_custom_call" | custom-call | tf_op jit(solution)/shard_map/update/pallas_call | solution.py:415
Async XLA Ops:
  0.0 138.8 %copy-start = (bf16[96,12288]{1,0:T(8,128)(2,1)S(1)}, bf16[96,12288]{1,0:T(8,128)(2,1)}, u32[]{:S(2)}) copy-start(bf16[96,12288]{1,0:T(8,128)(2,1)} %old_ref.1) | copy-start | bytes 7077892
  0.0 138.8 %copy-start.1 = (f32[384]{0:T(512)S(1)}, f32[384]{0:T(512)}, u32[]{:S(2)}) copy-start(f32[384]{0:T(512)} %virt_ref.1) | copy-start | bytes 4612
  0.0 138.8 %copy-start.2 = (f32[32]{0:T(128)S(1)}, f32[32]{0:T(128)}, u32[]{:S(2)}) copy-start(f32[32]{0:T(128)} %occ_ref.1) | copy-start | bytes 388

commit v9 on v8

--- a/solution.py
+++ b/solution.py
@@ -297,7 +297,7 @@
 
     def each_piece(t, remote_step, local_step):
         def piece(s, carry):
-            for src, dst, sent, landed, to_row, to_col in pieces(t, s):
+            for src, dst, sent, landed, to_row, to_col in pieces(t, s)[::-1]:
                 here = to_row * 16 + to_col == me
 
                 @pl.when(here)

time: 145 us -> 144 us (level)
  no operation moved by 1% of the time
where the time goes in v9:
time: 144 us; the launch traced here: 142 us
  Pallas kernels  142 us (99%)
    pallas_call x1, Pallas kernels, on_device(): pl.pallas_call(cycle_kernel, name='cycle', out_shape=(jax.ShapeDtypeStruc...  139 us
    pallas_call x1, Pallas kernels, on_device(): pl.pallas_call(update_kernel, name='update', out_shape=jax.ShapeDtypeStru...  3 us

profile of v9, /device:TPU:3, one launch (start us, length us, event | category | flops | bytes accessed | tf_op | source)
XLA Modules:
  0.0 142.0 jit_solution(9266636871170780436)
XLA Ops:
  0.0 0.0 copy-start
  0.0 0.0 copy-start.1
  0.0 0.0 copy-start.2
  0.0 138.9 %cycle.1 = (bf16[96,12288]{1,0:T(8,128)(2,1)S(1)}, bf16[96,12288]{1,0:T(8,128)(2,1)S(1)}) custom-call(s32[8,16]{1,0:T(8,128)} %bitcast.1, s32[384]{0:T(512)} %perm_ref.1, bf16[1536,384]{1,0:T(8,128)(2,1)} %w_ref.1, bf16[768,768]{1,0:T(8,128)(2,1)} %t_ref.1), custom_call_target="tpu_custom_call" | custom-call | tf_op jit(solution)/shard_map/cycle/pallas_call | solution.py:382
  139.0 0.0 copy-done
  139.0 0.0 copy-done.1
  139.0 0.0 copy-done.2
  139.0 3.0 %update.1 = f32[96,12288]{1,0:T(8,128)} custom-call(bf16[96,12288]{1,0:T(8,128)(2,1)S(1)} %get-tuple-element.7.rows_ref, bf16[96,12288]{1,0:T(8,128)(2,1)S(1)} %get-tuple-element.8.cols_ref, bf16[96,12288]{1,0:T(8,128)(2,1)S(1)} %copy-done, f32[384]{0:T(512)S(1)} %copy-done.1, f32[32]{0:T(128)S(1)} %copy-done.2), custom_call_target="tpu_custom_call" | custom-call | tf_op jit(solution)/shard_map/update/pallas_call | solution.py:415
Async XLA Ops:
  0.0 139.0 %copy-start = (bf16[96,12288]{1,0:T(8,128)(2,1)S(1)}, bf16[96,12288]{1,0:T(8,128)(2,1)}, u32[]{:S(2)}) copy-start(bf16[96,12288]{1,0:T(8,128)(2,1)} %old_ref.1) | copy-start | bytes 7077892
  0.0 139.0 %copy-start.1 = (f32[384]{0:T(512)S(1)}, f32[384]{0:T(512)}, u32[]{:S(2)}) copy-start(f32[384]{0:T(512)} %virt_ref.1) | copy-start | bytes 4612
  0.0 139.0 %copy-start.2 = (f32[32]{0:T(128)S(1)}, f32[32]{0:T(128)}, u32[]{:S(2)}) copy-start(f32[32]{0:T(128)} %occ_ref.1) | copy-start | bytes 388
